TPU v7x, 32 devices: a whole 2x2x4 slice. The times are simulated.
32 devices in a mesh: stream: 8 (over z, y), span: 4 (over x, core).
Axes of the slice: x: 2, y: 2, z: 4, core: 2. Of those that a mesh axis runs over, the one named last changes fastest.
Arguments:
- primal_populations: float32 [26, 64, 64, 128], P(None, 'stream', 'span'), may hold values from 0.01 to 0.8, as said below
- adjoint: float32 [26, 64, 64, 128], P(None, 'stream', 'span'), may hold values from -6 to 6
- solid: int32 [64, 64, 128], P('stream', 'span'), may hold values from 0 to 1, as said below
- links: int32 [3, 8, 9856], P(None, 'stream', 'span'), may hold values from 0 to 16384, as said below
Outputs:
- adjoint_next: float32 [26, 64, 64, 128], P(None, 'stream', 'span')
- sensitivity: float32 [128], replicated
Inputs may be any that keep to these rules, and one draw needn't show every extreme that they name: `primal_populations`: every entry is positive; in each cell the members 0..18 sum to between 0.5 and 1.5. Every fluid cell beside a solid cell lies on that solid cell's device. `links`: row 0 holds a fluid cell of the device's block, flattened as (x * 16 + y) * 128 + z over its 8 x 16 x 128 cells; row 1 a direction i of 1..18 for which that cell plus c_i is solid; row 2 the owning control point, which on the devices of span index p lies in p * 4 * 2 * 4 .. (p + 1) * 4 * 2 * 4 - 1. Every pair of a fluid cell and a direction toward a solid cell is listed once, on that cell's device. Unused slots hold cell 8 * 16 * 128, direction 0 and control point 128. On some device all 2464 slots are used, on another none.
All inputs are finite; a program needn't handle non-finite values.
Results may differ from a plain program's by a relative error of at most 0.0003.
Values sent between devices are 32-bit elements; how exact they have to be, the bound alone decides.
No kernel may reach another device: no remote copies, remote signals or barrier semaphores. Data moves between devices by JAX's collectives and lax.ppermute only.
A program may use at most 64 MiB of HBM per device.

v0:
```python
import jax
import jax.numpy as jnp
from jax import lax
from jax.sharding import PartitionSpec as P

SEGMENT_WIDTH = 6
PERIOD_PARTS = 4
SEGMENT_CONTROLS = 4
ITERS = 2


VELOCITY = (
    (0, 0, 0),
    (1, 0, 0),
    (-1, 0, 0),
    (0, 1, 0),
    (0, -1, 0),
    (0, 0, 1),
    (0, 0, -1),
    (1, 1, 0),
    (-1, -1, 0),
    (1, -1, 0),
    (-1, 1, 0),
    (1, 0, 1),
    (-1, 0, -1),
    (1, 0, -1),
    (-1, 0, 1),
    (0, 1, 1),
    (0, -1, -1),
    (0, 1, -1),
    (0, -1, 1),
)
WEIGHTS = (1.0 / 3.0,) + (1.0 / 18.0,) * 6 + (1.0 / 36.0,) * 12
QUADRATURE_HEAT = (0.25,) + (0.125,) * 6
OMEGA_FLOW = 1.0 / 0.6
OMEGA_CONDUCT = 1.25
SENS_SCALE = 0.125


def extended_2(cells, sides, width, closed):
    for axis, dim in sides:
        count = lax.axis_size(axis)
        ends = count if closed else count - 1
        head = lax.slice_in_dim(cells, 0, width, axis=dim)
        tail = lax.slice_in_dim(cells, cells.shape[dim] - width, cells.shape[dim], axis=dim)
        cells = jnp.concatenate(
            [
                lax.ppermute(tail, axis, [(i, (i + 1) % count) for i in range(ends)]),
                cells,
                lax.ppermute(head, axis, [((i + 1) % count, i) for i in range(ends)]),
            ],
            axis=dim,
        )
    return cells


def member_velocity(discrete_direction):
    if discrete_direction < 19:
        return VELOCITY[discrete_direction]
    return VELOCITY[discrete_direction - 19]


def member_opposite(discrete_direction):
    if discrete_direction >= 19:
        return 19 + member_opposite(discrete_direction - 19)
    if discrete_direction % 2 == 1:
        return discrete_direction + 1
    return discrete_direction - 1


def opposite_of(directions):
    return jnp.where(
        directions == 0, 0, jnp.where(directions % 2 == 1, directions + 1, directions - 1)
    )


def dot_velocity(velocity, speed_streamwise_first, speed_transverse_second, speed_vertical_third):
    total = jnp.zeros_like(speed_streamwise_first)
    for coefficient, component_speed in zip(
        velocity, (speed_streamwise_first, speed_transverse_second, speed_vertical_third)
    ):
        if coefficient != 0:
            total = total + float(coefficient) * component_speed
    return total


def hydrodynamic_sums(population_array):
    mass_per_volume = jnp.sum(population_array[:19], axis=0)
    energy_currents = [jnp.zeros_like(mass_per_volume) for dimension in range(3)]
    for discrete_direction in range(1, 19):
        for dimension in range(3):
            if VELOCITY[discrete_direction][dimension] != 0:
                energy_currents[dimension] = (
                    energy_currents[dimension]
                    + float(VELOCITY[discrete_direction][dimension])
                    * population_array[discrete_direction]
                )
    warmth_grid = jnp.sum(population_array[19:], axis=0)
    return (
        mass_per_volume,
        energy_currents[0] / mass_per_volume,
        energy_currents[1] / mass_per_volume,
        energy_currents[2] / mass_per_volume,
        warmth_grid,
    )


def perform_impact_step(
    gathered_neighbour_entries,
    mass_per_volume,
    speed_streamwise_first,
    speed_transverse_second,
    speed_vertical_third,
    warmth_grid,
):
    speeds = (speed_streamwise_first, speed_transverse_second, speed_vertical_third)
    square = (
        speed_streamwise_first * speed_streamwise_first
        + speed_transverse_second * speed_transverse_second
        + speed_vertical_third * speed_vertical_third
    )
    scalar_sum = jnp.zeros_like(mass_per_volume)
    moment_sum = [jnp.zeros_like(mass_per_volume) for dimension in range(3)]
    for discrete_direction in range(19):
        velocity = VELOCITY[discrete_direction]
        mapped_quantity = dot_velocity(
            velocity, speed_streamwise_first, speed_transverse_second, speed_vertical_third
        )
        weighted = WEIGHTS[discrete_direction] * gathered_neighbour_entries[discrete_direction]
        scalar_sum = scalar_sum + weighted * (
            1.0 + 3.0 * mapped_quantity + 4.5 * mapped_quantity * mapped_quantity - 1.5 * square
        )
        for dimension in range(3):
            moment_sum[dimension] = moment_sum[dimension] + weighted * (
                3.0 * velocity[dimension]
                + 9.0 * mapped_quantity * velocity[dimension]
                - 3.0 * speeds[dimension]
            )
    heat_sum = jnp.zeros_like(mass_per_volume)
    heat_vector = [jnp.zeros_like(mass_per_volume) for dimension in range(3)]
    for discrete_direction in range(7):
        velocity = VELOCITY[discrete_direction]
        weighted = (
            QUADRATURE_HEAT[discrete_direction]
            * gathered_neighbour_entries[19 + discrete_direction]
        )
        heat_sum = heat_sum + weighted * (
            1.0
            + 4.0
            * dot_velocity(
                velocity, speed_streamwise_first, speed_transverse_second, speed_vertical_third
            )
        )
        for dimension in range(3):
            if velocity[dimension] != 0:
                heat_vector[dimension] = (
                    heat_vector[dimension] + float(velocity[dimension]) * weighted
                )
    multiplier_coefficient = 4.0 * OMEGA_CONDUCT * warmth_grid / mass_per_volume
    pushed = [
        OMEGA_FLOW * moment_sum[dimension] + multiplier_coefficient * heat_vector[dimension]
        for dimension in range(3)
    ]
    offset = OMEGA_FLOW * scalar_sum - (
        pushed[0] * speed_streamwise_first
        + pushed[1] * speed_transverse_second
        + pushed[2] * speed_vertical_third
    )
    outputs = []
    for discrete_direction in range(19):
        outputs.append(
            (1.0 - OMEGA_FLOW) * gathered_neighbour_entries[discrete_direction]
            + offset
            + dot_velocity(VELOCITY[discrete_direction], pushed[0], pushed[1], pushed[2])
        )
    for discrete_direction in range(7):
        outputs.append(
            (1.0 - OMEGA_CONDUCT) * gathered_neighbour_entries[19 + discrete_direction]
            + OMEGA_CONDUCT * heat_sum
        )
    return jnp.stack(outputs)


def postimpact_populations(
    population_array,
    mass_per_volume,
    speed_streamwise_first,
    speed_transverse_second,
    speed_vertical_third,
    warmth_grid,
):
    square = (
        speed_streamwise_first * speed_streamwise_first
        + speed_transverse_second * speed_transverse_second
        + speed_vertical_third * speed_vertical_third
    )
    outputs = []
    for discrete_direction in range(19):
        mapped_quantity = dot_velocity(
            VELOCITY[discrete_direction],
            speed_streamwise_first,
            speed_transverse_second,
            speed_vertical_third,
        )
        maxwellian_target = (
            WEIGHTS[discrete_direction]
            * mass_per_volume
            * (1.0 + 3.0 * mapped_quantity + 4.5 * mapped_quantity * mapped_quantity - 1.5 * square)
        )
        outputs.append(
            population_array[discrete_direction]
            - OMEGA_FLOW * (population_array[discrete_direction] - maxwellian_target)
        )
    for discrete_direction in range(7):
        mapped_quantity = dot_velocity(
            VELOCITY[discrete_direction],
            speed_streamwise_first,
            speed_transverse_second,
            speed_vertical_third,
        )
        maxwellian_target = (
            QUADRATURE_HEAT[discrete_direction] * warmth_grid * (1.0 + 4.0 * mapped_quantity)
        )
        outputs.append(
            population_array[19 + discrete_direction]
            - OMEGA_CONDUCT * (population_array[19 + discrete_direction] - maxwellian_target)
        )
    return jnp.stack(outputs)


def shift_zero(section, offset_by, dimension):
    if offset_by == 0:
        return section
    length = section.shape[dimension]
    pad_shape = list(section.shape)
    pad_shape[dimension] = 1
    blank = jnp.zeros(pad_shape, section.dtype)
    if offset_by == 1:
        return jnp.concatenate(
            [lax.slice_in_dim(section, 1, length, axis=dimension), blank], axis=dimension
        )
    return jnp.concatenate(
        [blank, lax.slice_in_dim(section, 0, length - 1, axis=dimension)], axis=dimension
    )


def pull_whole(iterate_snapshot):
    rows_x = iterate_snapshot.shape[1]
    spanwise_rows = iterate_snapshot.shape[2]
    extended = extended_2(iterate_snapshot, (("stream", 1),), 1, True)
    extended = extended_2(extended, (("span", 2),), 1, False)
    planes = []
    for discrete_direction in range(26):
        velocity = member_velocity(discrete_direction)
        section = extended[
            discrete_direction,
            1 + velocity[0] : 1 + velocity[0] + rows_x,
            1 + velocity[1] : 1 + velocity[1] + spanwise_rows,
        ]
        planes.append(shift_zero(section, velocity[2], 2))
    return jnp.stack(planes)


def bounce_walls(
    gathered_neighbour_entries, iterate_snapshot, y_index, y_total, z_index, depth_cells
):
    planes = []
    for discrete_direction in range(26):
        velocity = member_velocity(discrete_direction)
        at_wall = None
        if velocity[1] == 1:
            at_wall = y_index == y_total - 1
        elif velocity[1] == -1:
            at_wall = y_index == 0
        if velocity[2] != 0:
            wall_z = z_index == depth_cells - 1 if velocity[2] == 1 else z_index == 0
            at_wall = wall_z if at_wall is None else at_wall | wall_z
        if at_wall is None:
            planes.append(gathered_neighbour_entries[discrete_direction])
        else:
            planes.append(
                jnp.where(
                    at_wall,
                    iterate_snapshot[member_opposite(discrete_direction)],
                    gathered_neighbour_entries[discrete_direction],
                )
            )
    return jnp.stack(planes)


def shards(primal_populations, adjoint, solid, links):
    members, rows_x, spanwise_rows, depth_cells = adjoint.shape
    cell_count = rows_x * spanwise_rows * depth_cells
    spanwise_count = lax.axis_size("span")
    stream_count = lax.axis_size("stream")
    span_index = lax.axis_index("span")
    y_index = span_index * spanwise_rows + lax.broadcasted_iota(jnp.int32, (1, spanwise_rows, 1), 1)
    z_index = lax.broadcasted_iota(jnp.int32, (1, 1, depth_cells), 2)
    (
        mass_per_volume,
        speed_streamwise_first,
        speed_transverse_second,
        speed_vertical_third,
        warmth_grid,
    ) = hydrodynamic_sums(primal_populations)
    liquid_occupied_sites = (1 - solid).astype(jnp.float32)
    cell_ids = links[0, 0]
    directions = links[1, 0]
    owner_parts = links[2, 0]
    usable = cell_ids < cell_count
    safe_cells = jnp.where(usable, cell_ids, 0)
    opposite = opposite_of(directions)
    axis_link = usable & (directions >= 1) & (directions <= 6)
    flow_slot = jnp.where(usable, directions, members)
    heat_slot = jnp.where(axis_link, 19 + directions, members)
    heat_source = jnp.where(axis_link, 19 + opposite, 0)
    periods = stream_count // PERIOD_PARTS
    span_share = PERIOD_PARTS * (spanwise_rows // (SEGMENT_WIDTH + 2)) * SEGMENT_CONTROLS
    iterate_snapshot = adjoint
    sensitivity = jnp.zeros((span_share * spanwise_count,), jnp.float32)
    for iteration in range(ITERS):
        flattened = iterate_snapshot.reshape(members, cell_count)
        flow_back = flattened[opposite, safe_cells]
        heat_back = 1.0 - flattened[heat_source, safe_cells]
        if iteration == ITERS - 1:
            gathered = primal_populations.reshape(members, cell_count)[:, safe_cells]
            link_density, link_x, link_y, link_z, link_heat = hydrodynamic_sums(gathered)
            post_state = postimpact_populations(
                gathered, link_density, link_x, link_y, link_z, link_heat
            )
            row_ids = lax.broadcasted_iota(jnp.int32, post_state.shape, 0)
            flow_pick = jnp.sum(jnp.where(row_ids == directions[None], post_state, 0.0), axis=0)
            heat_pick = jnp.sum(
                jnp.where(row_ids == 19 + directions[None], post_state, 0.0), axis=0
            )
            link_terms = jnp.where(usable, flow_pick * flow_back, 0.0) + jnp.where(
                axis_link, heat_pick * heat_back, 0.0
            )
            indicator = (
                owner_parts[:, None]
                == lax.broadcasted_iota(jnp.int32, (1, span_share * spanwise_count), 1)
            ).astype(jnp.float32)
            partial_value = jnp.dot(link_terms[None], indicator, precision=lax.Precision.HIGHEST)[0]
            assembled = lax.psum(partial_value, ("stream", "span"))
            sensitivity = assembled * (SENS_SCALE / periods)
        gathered_neighbour_entries = pull_whole(iterate_snapshot)
        gathered_neighbour_entries = bounce_walls(
            gathered_neighbour_entries,
            iterate_snapshot,
            y_index,
            spanwise_rows * spanwise_count,
            z_index,
            depth_cells,
        )
        flat_pull = gathered_neighbour_entries.reshape(members, cell_count)
        flat_pull = flat_pull.at[flow_slot, safe_cells].set(flow_back, mode="drop")
        flat_pull = flat_pull.at[heat_slot, safe_cells].set(heat_back, mode="drop")
        gathered_neighbour_entries = flat_pull.reshape(members, rows_x, spanwise_rows, depth_cells)
        iterate_snapshot = (
            perform_impact_step(
                gathered_neighbour_entries,
                mass_per_volume,
                speed_streamwise_first,
                speed_transverse_second,
                speed_vertical_third,
                warmth_grid,
            )
            * liquid_occupied_sites[None]
        )
    return (iterate_snapshot, sensitivity)


def solution(mesh):
    placed = (
        P(None, "stream", "span", None),
        P(None, "stream", "span", None),
        P("stream", "span", None),
        P(None, "stream", "span"),
    )
    return jax.shard_map(
        shards,
        mesh=mesh,
        in_specs=placed,
        out_specs=(P(None, "stream", "span", None), P()),
        check_vma=False,
    )
```

profile of v0, /device:TPU:1, one launch (start us, length us, event | category | flops | bytes accessed | tf_op | source)
XLA Modules:
  0.0 272.7 jit_solution(7783677678240438253)
XLA Ops:
  0.6 1.9 fusion.92
  2.5 2.1 collective-permute-start.1
  4.6 3.0 %collective-permute-start = (f32[26,1,16,128]{3,2,1,0:T(8,128)}, f32[26,1,16,128]{3,2,1,0:T(8,128)}, u32[]{:S(2)}, u32[]{:S(2)}) collective-permute-start(f32[26,1,16,128]{3,2,1,0:T(8,128)} %get-tuple-element.296), channel_id=1, source_target_pairs={{4,0},{8,4},{12,8},{16,12},{20,16},{24,20},{28,24},{0,28},{5,1},{9... | collective-permute-start | bytes 638984 | tf_op jit(solution)/shard_map/ppermute | solution.py:50
  7.6 1.5 fusion.85
  9.1 6.3 %copy.87 = f32[26,8,16,128]{0,3,2,1:T(8,128)} copy(f32[26,8,16,128]{3,2,1,0:T(8,128)} %param.4) | data formatting | bytes 3407872 | tf_op args[0]
  15.4 9.1 %gather_fusion.4 = f32[2464,26]{1,0:T(8,128)} fusion(f32[26,16384]{0,1:T(8,128)} %bitcast.359, s32[3072]{0:T(1024)S(1)} %pad_clamp_fusion), kind=kCustom, calls=%fused_computation.4 | custom fusion | bytes 522368 | tf_op jit(solution)/shard_map/gather | solution.py:326
  24.5 2.6 copy.88
  27.1 1.5 slice_reduce_fusion.3
  28.6 1.0 slice_reduce_fusion.2
  29.6 0.6 slice_reduce_fusion.4
  30.2 0.5 fusion.86
  30.7 0.6 fusion.87
  31.3 0.6 iota_compare_fusion.6
  32.0 0.7 slice_bitcast_fusion.19
  32.7 0.7 slice_reduce_fusion.1
  33.3 0.6 compare_reduce_fusion
  34.5 0.3 multiply_subtract_fusion.55
  34.7 0.4 multiply_subtract_fusion.44
  35.1 0.7 compare_select_fusion.1
  35.9 0.9 multiply_reduce_fusion
  37.1 1.2 copy.89
  38.4 19.3 %gather_fusion = f32[2464]{0:T(1024)S(1)} fusion(f32[26,16384]{1,0:T(8,128)S(1)} %bitcast.356, s32[2464]{0:T(1024)S(1)} %get-tuple-element.7), kind=kCustom, calls=%fused_computation | custom fusion | bytes 39424 | tf_op jit(solution)/shard_map/gather | solution.py:323
  57.7 19.3 %gather_fusion.1 = f32[2464]{0:T(1024)S(1)} fusion(f32[26,16384]{1,0:T(8,128)S(1)} %bitcast.357, s32[2464]{0:T(1024)S(1)} %get-tuple-element.6), kind=kCustom, calls=%fused_computation.1 | custom fusion | bytes 39424 | tf_op jit(solution)/shard_map/gather | solution.py:324
  77.0 0.4 stack.374
  77.7 1.0 constant_dynamic-update-slice_fusion.6
  78.7 0.5 constant_dynamic-update-slice_fusion.5
  79.2 1.0 constant_dynamic-update-slice_fusion.4
  80.3 4.1 %collective-permute-start.3 = (f32[26,10,1,128]{3,2,1,0:T(1,128)S(1)}, f32[26,10,1,128]{3,2,1,0:T(1,128)S(1)}, u32[]{:S(2)}, u32[]{:S(2)}) collective-permute-start(f32[26,10,1,128]{3,2,1,0:T(1,128)S(1)} %get-tuple-element.118), channel_id=1, source_target_pairs={{0,1},{1,2},{2,3},{4,5},{5,6},{6,7},{8,9},{9,10},{10,11},{12,13},{... | collective-permute-start | bytes 399368 | tf_op jit(solution)/shard_map/ppermute | solution.py:48
  84.5 1.9 collective-permute-start.2
  86.4 0.7 fusion.90
  87.2 0.7 fusion.89
  88.1 2.6 collective-permute-done.2
  91.1 0.7 bitcast_select_fusion
  91.8 0.8 pad_select_fusion.4
  92.7 8.3 %stack.317 = f32[26,16384]{1,0:T(8,128)} concatenate(f32[1,16384]{1,0:T(1,128)} %bitcast.530, f32[1,16384]{1,0:T(1,128)} %bitcast.550, f32[1,16384]{1,0:T(1,128)} %bitcast.552, f32[1,16384]{1,0:T(1,128)S(1)} %bitcast.517, f32[1,16384]{1,0:T(1,128)S(1)} %bitcast.506, f32[1,16384]{1,0:T(1,128)} %bitcast.567, f32[1,16384]{1,0:T(1,128)} %bitcast.566, f32[1,16384]{1,0:T(1,128)S(1)} %bitcast.516, ...), dimensions={0} | concatenate | bytes 3407872 | tf_op jit(solution)/shard_map/stack | solution.py:288
  101.0 1.7 reshape.3122
  102.7 13.0 %scatter_fusion = f32[425984]{0:T(1024)S(1)} fusion(f32[425984]{0:T(1024)S(1)} %reshape.3122, s32[2464]{0:T(1024)S(1)} %get-tuple-element.347, f32[2464]{0:T(1024)S(1)} %gather_fusion), kind=kCustom, calls=%fused_computation.5 | custom fusion | bytes 39424
  115.6 13.1 %scatter_fusion.1 = f32[425984]{0:T(1024)S(1)} fusion(f32[425984]{0:T(1024)S(1)} %scatter_fusion, s32[2464]{0:T(1024)S(1)} %get-tuple-element.346, f32[2464]{0:T(1024)S(1)} %broadcast_subtract_fusion.1), kind=kCustom, calls=%fused_computation.6 | custom fusion | bytes 39424
  129.2 1.2 copy-done.3
  130.4 1.1 constant_dynamic-update-slice_fusion.32
  132.2 1.2 copy-done.5
  133.4 5.3 %stack.372 = f32[26,16384]{1,0:T(8,128)} concatenate(f32[1,16384]{1,0:T(1,128)S(1)} %bitcast.410, f32[1,16384]{1,0:T(1,128)S(1)} %bitcast.496, f32[1,16384]{1,0:T(1,128)S(1)} %bitcast.497, f32[1,16384]{1,0:T(1,128)S(1)} %bitcast.498, f32[1,16384]{1,0:T(1,128)S(1)} %bitcast.499, f32[1,16384]{1,0:T(1,128)S(1)} %bitcast.500, f32[1,16384]{1,0:T(1,128)S(1)} %bitcast.501, ...), dimensions={0} | concatenate | bytes 3407872 | tf_op jit(solution)/shard_map/stack | solution.py:181
  138.7 1.8 broadcast_multiply_fusion
  140.5 19.3 %gather_fusion.3 = f32[2464]{0:T(1024)S(1)} fusion(f32[26,16384]{1,0:T(8,128)S(1)} %broadcast_multiply_fusion, s32[2464]{0:T(1024)S(1)} %get-tuple-element.6), kind=kCustom, calls=%fused_computation.3 | custom fusion | bytes 39424 | tf_op jit(solution)/shard_map/gather | solution.py:324
  159.7 19.3 %gather_fusion.2 = f32[2464]{0:T(1024)S(1)} fusion(f32[26,16384]{1,0:T(8,128)S(1)} %broadcast_multiply_fusion, s32[2464]{0:T(1024)S(1)} %get-tuple-element.7), kind=kCustom, calls=%fused_computation.2 | custom fusion | bytes 39424 | tf_op jit(solution)/shard_map/gather | solution.py:323
  179.0 1.7 broadcast_multiply_fusion.2
  180.8 1.6 collective-permute-start.4
  182.4 0.7 fusion.1
  183.1 37.8 %psum.7 = f32[128]{0:T(128)S(1)} all-reduce(f32[128]{0:T(128)S(1)} %fusion.1), channel_id=1, replica_groups=mesh['stream'=8,'span'=4] {'stream','span'}, use_global_device_ids=true, to_apply=%region_10.11 | all-reduce | flops 128 | bytes 1024 | tf_op jit(solution)/shard_map/psum | solution.py:344
  220.9 0.5 broadcast_multiply_fusion.10
  221.6 3.4 %collective-permute-start.6 = (f32[26,10,1,128]{3,2,1,0:T(1,128)S(1)}, f32[26,10,1,128]{3,2,1,0:T(1,128)S(1)}, u32[]{:S(2)}, u32[]{:S(2)}) collective-permute-start(f32[26,10,1,128]{3,2,1,0:T(1,128)S(1)} %get-tuple-element.117), channel_id=1, source_target_pairs={{1,0},{2,1},{3,2},{5,4},{6,5},{7,6},{9,8},{10,9},{11,10},{13,12},{... | collective-permute-start | bytes 399368 | tf_op jit(solution)/shard_map/ppermute | solution.py:50
  225.0 3.8 %collective-permute-start.7 = (f32[26,10,1,128]{3,2,1,0:T(1,128)S(1)}, f32[26,10,1,128]{3,2,1,0:T(1,128)S(1)}, u32[]{:S(2)}, u32[]{:S(2)}) collective-permute-start(f32[26,10,1,128]{3,2,1,0:T(1,128)S(1)} %get-tuple-element.116), channel_id=1, source_target_pairs={{0,1},{1,2},{2,3},{4,5},{5,6},{6,7},{8,9},{9,10},{10,11},{12,13},{... | collective-permute-start | bytes 399368 | tf_op jit(solution)/shard_map/ppermute | solution.py:48
  228.9 0.6 collective-permute-done.6
  229.6 0.7 maximum_bitcast_fusion.1
  230.3 0.4 collective-permute-done.7
  230.8 0.7 maximum_bitcast_fusion
  231.9 0.2 copy-done.15
  232.3 0.8 pad_select_fusion
  233.2 8.3 %stack.345 = f32[26,16384]{1,0:T(8,128)} concatenate(f32[1,16384]{1,0:T(1,128)S(1)} %bitcast.502, f32[1,16384]{1,0:T(1,128)} %bitcast.575, f32[1,16384]{1,0:T(1,128)S(1)} %bitcast.527, f32[1,16384]{1,0:T(1,128)} %bitcast.571, f32[1,16384]{1,0:T(1,128)} %bitcast.573, f32[1,16384]{1,0:T(1,128)} %bitcast.561, f32[1,16384]{1,0:T(1,128)S(1)} %bitcast.556, f32[1,16384]{1,0:T(1,128)S(1)} %bitcast.509, ...), dimensions={0} | concatenate | bytes 3407872 | tf_op jit(solution)/shard_map/stack | solution.py:288
  241.5 1.7 reshape.3130
  243.2 13.0 %scatter_fusion.2 = f32[425984]{0:T(1024)S(1)} fusion(f32[425984]{0:T(1024)S(1)} %reshape.3130, s32[2464]{0:T(1024)S(1)} %get-tuple-element.347, f32[2464]{0:T(1024)S(1)} %gather_fusion.2), kind=kCustom, calls=%fused_computation.7 | custom fusion | bytes 39424
  256.2 13.2 %scatter_fusion.3 = f32[425984]{0:T(1024)S(1)} fusion(f32[425984]{0:T(1024)S(1)} %scatter_fusion.2, s32[2464]{0:T(1024)S(1)} %get-tuple-element.346, f32[2464]{0:T(1024)S(1)} %get-tuple-element.337), kind=kCustom, calls=%fused_computation.8 | custom fusion | bytes 39424
  269.8 1.0 constant_dynamic-update-slice_fusion.58
  271.4 1.3 broadcast_multiply_fusion.1
  (157 shorter events, 4.9 us)
Async XLA Ops:
  2.5 75.2 %collective-permute-start.1 = (f32[26,1,16,128]{3,2,1,0:T(8,128)}, f32[26,1,16,128]{3,2,1,0:T(8,128)}, u32[]{:S(2)}, u32[]{:S(2)}) collective-permute-start(f32[26,1,16,128]{3,2,1,0:T(8,128)} %get-tuple-element.295), channel_id=1, source_target_pairs={{0,4},{4,8},{8,12},{12,16},{16,20},{20,24},{24,28},{28,0},{1,5},{5... | collective-permute-start | bytes 638984 | tf_op jit(solution)/shard_map/ppermute | solution.py:48
  4.6 74.6 %collective-permute-start = (f32[26,1,16,128]{3,2,1,0:T(8,128)}, f32[26,1,16,128]{3,2,1,0:T(8,128)}, u32[]{:S(2)}, u32[]{:S(2)}) collective-permute-start(f32[26,1,16,128]{3,2,1,0:T(8,128)} %get-tuple-element.296), channel_id=1, source_target_pairs={{4,0},{8,4},{12,8},{16,12},{20,16},{24,20},{28,24},{0,28},{5,1},{9... | collective-permute-start | bytes 638984 | tf_op jit(solution)/shard_map/ppermute | solution.py:50
  15.4 17.2 %copy-start.2 = (f32[26,8,16,128]{3,2,1,0:T(8,128)S(1)}, f32[26,8,16,128]{3,2,1,0:T(8,128)}, u32[]{:S(2)}) copy-start(f32[26,8,16,128]{3,2,1,0:T(8,128)} %param.4) | copy-start | bytes 5111812
  24.5 5.1 %copy-start.9 = (s32[3,1,2464]{2,1,0:T(1,128)S(1)}, s32[3,1,2464]{2,1,0:T(1,128)}, u32[]{:S(2)}) copy-start(s32[3,1,2464]{2,1,0:T(1,128)} %param.7) | copy-start | bytes 88708
  24.5 7.4 %copy-start = (f32[26,8,16,128]{3,2,1,0:T(8,128)S(1)}, f32[26,8,16,128]{3,2,1,0:T(8,128)}, u32[]{:S(2)}) copy-start(f32[26,8,16,128]{3,2,1,0:T(8,128)} %param.5) | copy-start | bytes 5111812
  30.2 3.7 %copy-start.13 = (f32[2464]{0:T(1024)S(1)}, f32[2464]{0:T(1024)}, u32[]{:S(2)}) copy-start(f32[2464]{0:T(1024)} %slice_reduce_fusion.3) | copy-start | bytes 29572
  30.2 3.7 %copy-start.4 = (f32[2464,26]{0,1:T(8,128)S(1)}, f32[2464,26]{0,1:T(8,128)}, u32[]{:S(2)}) copy-start(f32[2464,26]{0,1:T(8,128)} %copy.88) | copy-start | bytes 768772
  31.9 4.8 %copy-start.10 = (s32[2464,1]{0,1:T(1,128)S(1)}, s32[2464,1]{0,1:T(1,128)}, u32[]{:S(2)}) copy-start(s32[2464,1]{0,1:T(1,128)} %get-tuple-element.91) | copy-start | bytes 29572
  31.9 4.8 %copy-start.11 = (s32[2464,1]{0,1:T(1,128)S(1)}, s32[2464,1]{0,1:T(1,128)}, u32[]{:S(2)}) copy-start(s32[2464,1]{0,1:T(1,128)} %get-tuple-element.335) | copy-start | bytes 29572
  31.9 4.8 %copy-start.29 = (s32[2]{0:T(128)S(1)}, s32[2]{0:T(128)}, u32[]{:S(2)}) copy-start(s32[2]{0:T(128)} %constant.212) | copy-start | bytes 28
  57.6 19.3 %copy-start.12 = (s32[8,16,128]{2,1,0:T(8,128)S(1)}, s32[8,16,128]{2,1,0:T(8,128)}, u32[]{:S(2)}) copy-start(s32[8,16,128]{2,1,0:T(8,128)} %param.6) | copy-start | bytes 196612
  57.6 19.9 %copy-start.18 = (pred[16]{0:T(512)(128)(4,1)S(1)}, pred[16]{0:T(512)(128)(4,1)}, u32[]{:S(2)}) copy-start(pred[16]{0:T(512)(128)(4,1)} %fusion.86) | copy-start | bytes 52
  57.6 19.9 %copy-start.20 = (pred[16]{0:T(512)(128)(4,1)S(1)}, pred[16]{0:T(512)(128)(4,1)}, u32[]{:S(2)}) copy-start(pred[16]{0:T(512)(128)(4,1)} %fusion.87) | copy-start | bytes 52
  57.7 19.9 %copy-start.23 = (pred[128]{0:T(512)(128)(4,1)S(1)}, pred[128]{0:T(512)(128)(4,1)}, u32[]{:S(2)}) copy-start(pred[128]{0:T(512)(128)(4,1)} %get-tuple-element.344) | copy-start | bytes 388
  57.7 19.9 %copy-start.26 = (pred[128]{0:T(512)(128)(4,1)S(1)}, pred[128]{0:T(512)(128)(4,1)}, u32[]{:S(2)}) copy-start(pred[128]{0:T(512)(128)(4,1)} %get-tuple-element.345) | copy-start | bytes 388
  76.9 1.7 copy-start.1
  77.7 13.4 %copy-start.14 = (pred[16,128]{1,0:T(8,128)(4,1)}, pred[16,128]{1,0:T(8,128)(4,1)S(1)}, u32[]{:S(2)}) copy-start(pred[16,128]{1,0:T(8,128)(4,1)S(1)} %get-tuple-element.343) | copy-start | bytes 6148
  80.3 7.6 %collective-permute-start.3 = (f32[26,10,1,128]{3,2,1,0:T(1,128)S(1)}, f32[26,10,1,128]{3,2,1,0:T(1,128)S(1)}, u32[]{:S(2)}, u32[]{:S(2)}) collective-permute-start(f32[26,10,1,128]{3,2,1,0:T(1,128)S(1)} %get-tuple-element.118), channel_id=1, source_target_pairs={{0,1},{1,2},{2,3},{4,5},{5,6},{6,7},{8,9},{9,10},{10,11},{12,13},{... | collective-permute-start | bytes 399368 | tf_op jit(solution)/shard_map/ppermute | solution.py:48
  84.5 6.3 %collective-permute-start.2 = (f32[26,10,1,128]{3,2,1,0:T(1,128)S(1)}, f32[26,10,1,128]{3,2,1,0:T(1,128)S(1)}, u32[]{:S(2)}, u32[]{:S(2)}) collective-permute-start(f32[26,10,1,128]{3,2,1,0:T(1,128)S(1)} %get-tuple-element.119), channel_id=1, source_target_pairs={{1,0},{2,1},{3,2},{5,4},{6,5},{7,6},{9,8},{10,9},{11,10},{13,12},{... | collective-permute-start | bytes 399368 | tf_op jit(solution)/shard_map/ppermute | solution.py:50
  87.8 2.9 %copy-start.21 = (pred[16]{0:T(512)(128)(4,1)S(1)}, pred[16]{0:T(512)(128)(4,1)}, u32[]{:S(2)}) copy-start(pred[16]{0:T(512)(128)(4,1)} %fusion.87) | copy-start | bytes 52
  88.1 3.7 %copy-start.7 = (f32[8,16,128]{2,1,0:T(8,128)S(1)}, f32[8,16,128]{2,1,0:T(8,128)}, u32[]{:S(2)}) copy-start(f32[8,16,128]{2,1,0:T(8,128)} %get-tuple-element.290) | copy-start | bytes 196612
  88.1 3.7 %copy-start.24 = (pred[128]{0:T(512)(128)(4,1)S(1)}, pred[128]{0:T(512)(128)(4,1)}, u32[]{:S(2)}) copy-start(pred[128]{0:T(512)(128)(4,1)} %get-tuple-element.344) | copy-start | bytes 388
  88.1 3.7 %copy-start.27 = (pred[128]{0:T(512)(128)(4,1)S(1)}, pred[128]{0:T(512)(128)(4,1)}, u32[]{:S(2)}) copy-start(pred[128]{0:T(512)(128)(4,1)} %get-tuple-element.345) | copy-start | bytes 388
  91.8 0.8 copy-start.8
  128.9 1.5 copy-start.3
  128.9 1.4 copy-start.6
  132.2 1.2 copy-start.5
  179.0 3.4 %copy-start.16 = (pred[2464]{0:T(1024)(128)(4,1)S(1)}, pred[2464]{0:T(1024)(128)(4,1)}, u32[]{:S(2)}) copy-start(pred[2464]{0:T(1024)(128)(4,1)} %compare_reduce_fusion) | copy-start | bytes 7396
  179.0 3.4 %copy-start.17 = (s32[2464]{0:T(1024)S(1)}, s32[2464]{0:T(1024)}, u32[]{:S(2)}) copy-start(s32[2464]{0:T(1024)} %get-tuple-element.4) | copy-start | bytes 29572
  180.8 40.7 %collective-permute-start.4 = (f32[26,1,16,128]{3,2,1,0:T(8,128)S(1)}, f32[26,1,16,128]{3,2,1,0:T(8,128)S(1)}, u32[]{:S(2)}, u32[]{:S(2)}) collective-permute-start(f32[26,1,16,128]{3,2,1,0:T(8,128)S(1)} %get-tuple-element.222), channel_id=1, source_target_pairs={{4,0},{8,4},{12,8},{16,12},{20,16},{24,20},{28,24},{0,28},{5,1},{9... | collective-permute-start | bytes 638984 | tf_op jit(solution)/shard_map/ppermute | solution.py:50
  182.4 39.0 %collective-permute-start.5 = (f32[26,1,16,128]{3,2,1,0:T(8,128)S(1)}, f32[26,1,16,128]{3,2,1,0:T(8,128)S(1)}, u32[]{:S(2)}, u32[]{:S(2)}) collective-permute-start(f32[26,1,16,128]{3,2,1,0:T(8,128)S(1)} %get-tuple-element.221), channel_id=1, source_target_pairs={{0,4},{4,8},{8,12},{12,16},{16,20},{20,24},{24,28},{28,0},{1,5},{5... | collective-permute-start | bytes 638984 | tf_op jit(solution)/shard_map/ppermute | solution.py:48
  221.6 8.0 %copy-start.22 = (pred[16]{0:T(512)(128)(4,1)S(1)}, pred[16]{0:T(512)(128)(4,1)}, u32[]{:S(2)}) copy-start(pred[16]{0:T(512)(128)(4,1)} %fusion.87) | copy-start | bytes 52
  221.6 7.9 %collective-permute-start.6 = (f32[26,10,1,128]{3,2,1,0:T(1,128)S(1)}, f32[26,10,1,128]{3,2,1,0:T(1,128)S(1)}, u32[]{:S(2)}, u32[]{:S(2)}) collective-permute-start(f32[26,10,1,128]{3,2,1,0:T(1,128)S(1)} %get-tuple-element.117), channel_id=1, source_target_pairs={{1,0},{2,1},{3,2},{5,4},{6,5},{7,6},{9,8},{10,9},{11,10},{13,12},{... | collective-permute-start | bytes 399368 | tf_op jit(solution)/shard_map/ppermute | solution.py:50
  225.0 5.8 %collective-permute-start.7 = (f32[26,10,1,128]{3,2,1,0:T(1,128)S(1)}, f32[26,10,1,128]{3,2,1,0:T(1,128)S(1)}, u32[]{:S(2)}, u32[]{:S(2)}) collective-permute-start(f32[26,10,1,128]{3,2,1,0:T(1,128)S(1)} %get-tuple-element.116), channel_id=1, source_target_pairs={{0,1},{1,2},{2,3},{4,5},{5,6},{6,7},{8,9},{9,10},{10,11},{12,13},{... | collective-permute-start | bytes 399368 | tf_op jit(solution)/shard_map/ppermute | solution.py:48
  228.9 1.9 copy-start.19
  231.5 0.7 copy-start.15
  231.6 0.7 copy-start.25
  231.6 0.7 copy-start.28
where the time goes:
time: 274 us; the launch traced here: 273 us
  local copies, waits for them, and re-layouts  185 us (68%)
  blocking collectives  37.8 us (14%)
  other arithmetic  23.6 us (9%)
  starting transfers between devices  20 us (7%)
  waiting for transfers between devices  3.71 us (1%)
    unnamed x71, local copies, waits for them, and re-layouts  67.5 us
    gather x2, local copies, waits for them, and re-layouts, shards(): heat_back = 1.0 - flattened[heat_source, safe_cells]  38.5 us
    gather x2, local copies, waits for them, and re-layouts, shards(): flow_back = flattened[opposite, safe_cells]  38.5 us
    psum x1, blocking collectives, shards(): assembled = lax.psum(partial_value, ('stream', 'span'))  37.8 us
    another operation x2, local copies, waits for them, and re-layouts, bounce_walls(): return jnp.stack(planes)  16.6 us
    gather x2, local copies, waits for them, and re-layouts, shards(): gathered = primal_populations.reshape(members, cell_count)[:, safe_cells]  11.7 us
    ppermute x4, starting transfers between devices, extended_2(): lax.ppermute(head, axis, [((i + 1) % count, i) for i in range(ends)])  9.99 us
    ppermute x4, starting transfers between devices, extended_2(): lax.ppermute(tail, axis, [(i, (i + 1) % count) for i in range(ends)])  9.98 us
  transfers between devices with their start and end apart: 8, of which 3 were waited for; matrix products, arithmetic and copies ran while one was open for 27% of the time, Pallas kernels for 0%

commit v1 on v0

v1 whole, which is shorter than its diff:
```python
import functools

import jax
import jax.numpy as jnp
from jax import lax
from jax.experimental import pallas as pl
from jax.experimental.pallas import tpu as pltpu
from jax.sharding import PartitionSpec as P

SEGMENT_WIDTH = 6
PERIOD_PARTS = 4
SEGMENT_CONTROLS = 4
SENS_SCALE = 0.125

VELOCITY = (
    (0, 0, 0),
    (1, 0, 0),
    (-1, 0, 0),
    (0, 1, 0),
    (0, -1, 0),
    (0, 0, 1),
    (0, 0, -1),
    (1, 1, 0),
    (-1, -1, 0),
    (1, -1, 0),
    (-1, 1, 0),
    (1, 0, 1),
    (-1, 0, -1),
    (1, 0, -1),
    (-1, 0, 1),
    (0, 1, 1),
    (0, -1, -1),
    (0, 1, -1),
    (0, -1, 1),
)
C = VELOCITY + VELOCITY[:7]
WEIGHTS = (1.0 / 3.0,) + (1.0 / 18.0,) * 6 + (1.0 / 36.0,) * 12
HEAT = (0.25,) + (0.125,) * 6
OMEGA_F = 1.0 / 0.6
OMEGA_T = 1.25
MEMBERS = 26


def opp(m):
    if m >= 19:
        return 19 + opp(m - 19)
    return 0 if m == 0 else m + 1 if m % 2 else m - 1


def movers(axis, sign):
    return [m for m in range(MEMBERS) if C[m][axis] == sign]


XP, XM, YP, YM = movers(0, 1), movers(0, -1), movers(1, 1), movers(1, -1)
FACE = len(XP)

GROUP, BITS = 4, 6
GROUPS = -(-18 // GROUP)


def place(i):
    return (i - 1) // GROUP, BITS * ((i - 1) % GROUP)


def plus(*terms):
    terms = [t for t in terms if t is not None]
    return functools.reduce(lambda a, b: a + b, terms) if terms else None


def minus(a, b):
    if b is None:
        return a
    return -b if a is None else a - b


def times(c, a):
    return None if a is None or c is None else c * a


def collide(b, u, coef, fluid, wanted):
    g = b.get
    a = {i: plus(g(i), g(i + 1)) for i in range(1, 19, 2)}
    d = {i: minus(g(i), g(i + 1)) for i in range(1, 19, 2)}
    w0, w1, w2 = WEIGHTS[0], WEIGHTS[1], WEIGHTS[7]
    xy, xz, yz = plus(a[7], a[9]), plus(a[11], a[13]), plus(a[15], a[17])
    s0 = plus(times(w0, g(0)), times(w1, plus(a[1], a[3], a[5])), times(w2, plus(xy, xz, yz)))
    s1 = [
        plus(times(w1, d[1]), times(w2, plus(d[7], d[9], d[11], d[13]))),
        plus(times(w1, d[3]), times(w2, plus(minus(d[7], d[9]), d[15], d[17]))),
        plus(times(w1, d[5]), times(w2, plus(minus(d[11], d[13]), minus(d[15], d[17])))),
    ]
    sxx = plus(times(w1, a[1]), times(w2, plus(xy, xz)))
    syy = plus(times(w1, a[3]), times(w2, plus(xy, yz)))
    szz = plus(times(w1, a[5]), times(w2, plus(xz, yz)))
    sxy = times(w2, minus(a[7], a[9]))
    sxz = times(w2, minus(a[11], a[13]))
    syz = times(w2, minus(a[15], a[17]))
    rows = ((sxx, sxy, sxz), (sxy, syy, syz), (sxz, syz, szz))
    s2u = [plus(*(times(e, v) for e, v in zip(row, u))) for row in rows]
    dot = lambda p, q: plus(*(times(e, v) for e, v in zip(p, q)))
    uu = u[0] * u[0] + u[1] * u[1] + u[2] * u[2]
    m0 = plus(times(1.0 - 1.5 * uu, s0), times(3.0, dot(s1, u)), times(4.5, dot(s2u, u)))
    m = [
        minus(plus(times(3.0, s1[k]), times(9.0, s2u[k])), times(3.0, times(u[k], s0)))
        for k in range(3)
    ]
    t0 = plus(
        times(HEAT[0], g(19)), times(HEAT[1], plus(*(g(20 + k) for k in range(6))))
    )
    t1 = [times(HEAT[1], minus(g(20 + 2 * k), g(21 + 2 * k))) for k in range(3)]
    s = plus(t0, times(4.0, dot(t1, u)))
    p = [plus(times(OMEGA_F, m[k]), times(coef, t1[k])) for k in range(3)]
    base = times(fluid, minus(times(OMEGA_F, m0), dot(p, u)))
    p = [times(fluid, e) for e in p]
    relax_f, relax_t = (1.0 - OMEGA_F) * fluid, (1.0 - OMEGA_T) * fluid
    heat = times(fluid, times(OMEGA_T, s))
    out = {}
    for i in wanted:
        if i < 19:
            value = plus(times(relax_f, g(i)), base)
            for k in range(3):
                if C[i][k] == 1:
                    value = plus(value, p[k])
                elif C[i][k] == -1:
                    value = minus(value, p[k])
            out[i] = value
        else:
            out[i] = plus(times(relax_t, g(i)), heat)
    return out


def wall_of(m, rows, lanes, y_first, y_last):
    mask = None
    if C[m][1] != 0:
        mask = rows == (y_last if C[m][1] == 1 else y_first)
    if C[m][2] != 0:
        edge = lanes == (lanes.shape[1] - 1 if C[m][2] == 1 else 0)
        mask = edge if mask is None else mask | edge
    return mask


def shifted(slab, m, fill, rows):
    count, width = slab.shape
    if C[m][1] == 1:
        slab = jnp.where(rows == count - 1, fill, pltpu.roll(slab, count - 1, 0))
    elif C[m][1] == -1:
        slab = jnp.where(rows == 0, fill, pltpu.roll(slab, 1, 0))
    if C[m][2] != 0:
        slab = pltpu.roll(slab, width - 1 if C[m][2] == 1 else 1, 1)
    return slab


def bounce(m, own, pulled, link, wall):
    pulled = jnp.zeros_like(own) if pulled is None else pulled
    if m < 19:
        return jnp.where(link if wall is None else link | wall, own, pulled)
    if wall is not None:
        pulled = jnp.where(wall, own, pulled)
    return jnp.where(link, 1.0 - own, pulled)


def link_mask(packed, x, m):
    group, low = place(m if m < 19 else m - 19)
    return (packed[group, x] & (((1 << BITS) - 1) << low)) != 0


def indices(shape):
    return (
        lax.broadcasted_iota(jnp.int32, shape, 0),
        lax.broadcasted_iota(jnp.int32, shape, 1),
    )


def pick(even, first, second):
    return jnp.where(even, first, second)


SPAN_EVEN, STREAM_EVEN, Y_FIRST, Y_LAST, CONTROL = range(5)


def pack_span_kernel(info, field, out_a, out_b, lo, hi, sems):
    rows = field.shape[2]
    copies = []
    for k in range(FACE):
        copies.append(pltpu.make_async_copy(field.at[YP[k], :, 0], lo.at[k], sems.at[k]))
        copies.append(
            pltpu.make_async_copy(field.at[YM[k], :, rows - 1], hi.at[k], sems.at[FACE + k])
        )
    for copy in copies:
        copy.start()
    for copy in copies:
        copy.wait()
    even = info[SPAN_EVEN] == 1
    for k in range(FACE):
        out_a[k] = pick(even, hi[k], lo[k])
        out_b[k] = pick(even, lo[k], hi[k])
    out_a[FACE] = jnp.zeros_like(out_a[FACE])
    out_b[FACE] = jnp.zeros_like(out_b[FACE])


def prepare_kernel(info, primal, solid, links, state, packed, span_of, slots):
    count_x, count_y, depth = solid.shape
    cells = count_x * count_y * depth
    for x in range(count_x):
        f = [primal[m, x] for m in range(MEMBERS)]
        rho = plus(*f[:19])
        inverse = 1.0 / rho
        momentum = [
            minus(plus(*(f[i] for i in range(1, 19) if C[i][k] == 1)),
                  plus(*(f[i] for i in range(1, 19) if C[i][k] == -1)))
            for k in range(3)
        ]
        theta = plus(*f[19:])
        for k in range(3):
            state[k, x] = momentum[k] * inverse
        state[3, x] = (4.0 * OMEGA_T) * theta * inverse
        state[4, x] = (1 - solid[x]).astype(jnp.float32)
        state[5, x] = rho
        state[6, x] = theta
    given = links.shape[2]
    slots[...] = jnp.full(slots.shape, cells, jnp.int32)
    for k in range(3):
        slots[k : k + 1, 0:given] = links[k]
    cell, direction = slots[0:1, :], slots[1:2, :]
    control = slots[2:3, :] - info[CONTROL]
    used = cell < cells
    span_of[0] = jnp.min(jnp.where(used, control, 1 << 20))
    span_of[1] = jnp.max(jnp.where(used, control, -1))
    total = slots.shape[1]
    column = lax.shift_right_logical(cell, depth.bit_length() - 1)
    height = cell & (depth - 1)
    columns = count_x * count_y
    on_column = lax.broadcasted_iota(jnp.int32, (columns, total), 0) == column
    on_height = jnp.where(
        (lax.broadcasted_iota(jnp.int32, (depth, total), 0) == height) & used, 1.0, 0.0
    ).astype(jnp.bfloat16)
    for group in range(GROUPS):
        code = jnp.zeros((1, total), jnp.float32)
        for i in range(1, 19):
            if place(i)[0] == group:
                value = (control + 1).astype(jnp.float32) * float(1 << place(i)[1])
                code = jnp.where(direction == i, value, code)
        left = jnp.where(on_column, code, 0.0).astype(jnp.bfloat16)
        dense = lax.dot_general(
            left, on_height, (((1,), (1,)), ((), ())), preferred_element_type=jnp.float32
        )
        packed[group] = dense.astype(jnp.int32).reshape(count_x, count_y, depth)


def message_rows(count_y):
    return (2 * FACE + 5) * count_y + 8


def gather_pull(field, halo_lo, halo_hi, x, m, rows, beyond_lo=None, beyond_hi=None):
    count_x = halo_lo.shape[1] if hasattr(halo_lo, "shape") else 0
    at = x + C[m][0]
    if at < 0 or at >= count_x:
        beyond = beyond_lo if at < 0 else beyond_hi
        if beyond is None:
            return None
        slab, fill = beyond(m)
    else:
        slab = field(m, at)
        fill = None
        if C[m][1] == 1:
            fill = halo_hi[YP.index(m), at : at + 1]
        elif C[m][1] == -1:
            fill = halo_lo[YM.index(m), at : at + 1]
    return shifted(slab, m, fill, rows)


def advance_slab(field, halo_lo, halo_hi, state, packed, x, info, beyond_lo=None, beyond_hi=None):
    rows, lanes = indices(state.shape[2:])
    b = {0: field(0, x), 19: field(19, x)}
    for m in range(MEMBERS):
        if m in (0, 19):
            continue
        pulled = gather_pull(field, halo_lo, halo_hi, x, m, rows, beyond_lo, beyond_hi)
        wall = wall_of(m, rows, lanes, info[Y_FIRST], info[Y_LAST])
        b[m] = bounce(m, field(opp(m), x), pulled, link_mask(packed, x, m), wall)
    u = [state[k, x] for k in range(3)]
    return collide(b, u, state[3, x], state[4, x], range(MEMBERS))


def select_halos(even, recv_a, recv_b, lo, hi):
    hi[...] = pick(even, recv_a[...], recv_b[...])
    lo[...] = pick(even, recv_b[...], recv_a[...])


def edge_kernel(info, adjoint, recv_a, recv_b, state, packed, edge, out_a, out_b, lo, hi):
    count_x, count_y = state.shape[1:3]
    select_halos(info[SPAN_EVEN] == 1, recv_a, recv_b, lo, hi)
    field = lambda m, x: adjoint[m, x]
    even = info[STREAM_EVEN] == 1
    for side, x, sent, flagged in ((0, 0, XP, XM), (1, count_x - 1, XM, XP)):
        out = advance_slab(field, lo, hi, state, packed, x, info)
        for m in range(MEMBERS):
            edge[side, m] = out[m]
        flags = state[4, x].astype(jnp.int32)
        for k, m in enumerate(flagged[: FACE - 1]):
            flags = flags + jnp.where(link_mask(packed, x, m), 2 << k, 0)
        parts = [adjoint[m, x] for m in sent] + [out[m] for m in sent]
        parts += [state[k, x] for k in range(4)] + [flags.astype(jnp.float32)]
        down = [m for m in sent if C[m][1] == -1][0]
        up = [m for m in sent if C[m][1] == 1][0]
        below, above = lo[YM.index(down), x : x + 1], hi[YP.index(up), x : x + 1]
        tail = jnp.concatenate(
            [below, above, jnp.zeros((6, below.shape[1]), jnp.float32)], axis=0
        )
        first = even if side == 1 else jnp.logical_not(even)

        def write(target):
            for k, part in enumerate(parts):
                target[k * count_y : (k + 1) * count_y] = part
            target[len(parts) * count_y : len(parts) * count_y + 8] = tail

        @pl.when(first)
        def _():
            write(out_a)

        @pl.when(jnp.logical_not(first))
        def _():
            write(out_b)


def interior_kernel(info, adjoint, recv_a, recv_b, state, packed, inner, lo, hi):
    count_x = state.shape[1]
    select_halos(info[SPAN_EVEN] == 1, recv_a, recv_b, lo, hi)
    field = lambda m, x: adjoint[m, x]
    for x in range(1, count_x - 1):
        out = advance_slab(field, lo, hi, state, packed, x, info)
        for m in range(MEMBERS):
            inner[m, x - 1] = out[m]


def correct_kernel(
    info, adjoint, span_a, span_b, recv_a, recv_b, state, packed, edge, inner,
    fixed, ring, out_a, out_b, lo, hi, message, send,
):
    count_x, count_y = state.shape[1:3]
    select_halos(info[SPAN_EVEN] == 1, span_a, span_b, lo, hi)
    even = info[STREAM_EVEN] == 1
    message[1] = pick(even, recv_a[...], recv_b[...])
    message[0] = pick(even, recv_b[...], recv_a[...])
    rows, lanes = indices(state.shape[2:])
    for side, x, came, went in ((0, 0, XM, XP), (1, count_x - 1, XP, XM)):
        part = lambda k: message[side, k * count_y : (k + 1) * count_y]
        tail = (2 * FACE + 5) * count_y
        b = {}
        for k, m in enumerate(came):
            row = tail if C[m][1] == -1 else tail + 1
            fill = message[side, row : row + 1] if C[m][1] != 0 else None
            pulled = shifted(part(k), m, fill, rows)
            blocked = link_mask(packed, x, m)
            wall = wall_of(m, rows, lanes, info[Y_FIRST], info[Y_LAST])
            blocked = blocked if wall is None else blocked | wall
            b[m] = jnp.where(blocked, 0.0, pulled)
        u = [state[k, x] for k in range(3)]
        out = collide(b, u, state[3, x], state[4, x], range(MEMBERS))
        for m in range(MEMBERS):
            fixed[side, m] = edge[side, m] + out[m]
        u = [part(2 * FACE + k) for k in range(3)]
        flags = part(2 * FACE + 4).astype(jnp.int32)
        b = {}
        for k, m in enumerate(went):
            fill = None
            if C[m][1] == 1:
                fill = hi[YP.index(m), x : x + 1]
            elif C[m][1] == -1:
                fill = lo[YM.index(m), x : x + 1]
            pulled = shifted(adjoint[m, x], m, fill, rows)
            blocked = (flags & (2 << (k % (FACE - 1)))) != 0
            wall = wall_of(m, rows, lanes, info[Y_FIRST], info[Y_LAST])
            blocked = blocked if wall is None else blocked | wall
            b[m] = jnp.where(blocked, 0.0, pulled)
        fluid = (flags & 1).astype(jnp.float32)
        out = collide(b, u, part(2 * FACE + 3), fluid, came)
        for k, m in enumerate(came):
            ring[side, k] = part(FACE + k) + out[m]
    last = count_y - 1
    for side, group, row in ((0, YP, 0), (1, YM, last)):
        for k, m in enumerate(group):
            send[side, k, 0:1] = fixed[0, m, row : row + 1]
            send[side, k, count_x - 1 : count_x] = fixed[1, m, row : row + 1]
            for x in range(1, count_x - 1):
                send[side, k, x : x + 1] = inner[m, x - 1, row : row + 1]
        send[side, FACE] = jnp.zeros((count_x, state.shape[3]), jnp.float32)
        for end, came in ((0, XM), (1, XP)):
            m = [e for e in came if e in group][0]
            send[side, FACE, end : end + 1] = ring[end, came.index(m), row : row + 1]
    span_even = info[SPAN_EVEN] == 1
    out_a[...] = pick(span_even, send[1], send[0])
    out_b[...] = pick(span_even, send[0], send[1])


CHUNK = 4


def sensitivity_kernel(info, span_of, primal, state, packed, fixed, inner, out, values, owners, acc):
    count_x, count_y, depth = state.shape[1:]

    def field(m, x):
        if x == 0 or x == count_x - 1:
            return fixed[0 if x == 0 else 1, m]
        return inner[m, x - 1]

    for x in range(count_x):
        u = [state[k, x] for k in range(3)]
        rho, theta = state[5, x], state[6, x]
        base = 1.0 - 1.5 * (u[0] * u[0] + u[1] * u[1] + u[2] * u[2])
        for i in range(1, 19):
            cu = None
            for k in range(3):
                cu = plus(cu, u[k]) if C[i][k] == 1 else minus(cu, u[k]) if C[i][k] == -1 else cu
            target = (OMEGA_F * WEIGHTS[i]) * rho * (base + cu * (3.0 + 4.5 * cu))
            value = ((1.0 - OMEGA_F) * primal[i, x] + target) * field(opp(i), x)
            if i <= 6:
                target = (OMEGA_T * HEAT[i]) * theta * (1.0 + 4.0 * cu)
                heat = (1.0 - OMEGA_T) * primal[19 + i, x] + target
                value = value + heat * (1.0 - field(19 + opp(i), x))
            group, low = place(i)
            owner = lax.shift_right_logical(packed[group, x], low) & ((1 << BITS) - 1)
            at = ((i - 1) * count_x + x) * count_y
            values[at : at + count_y] = value
            owners[at : at + count_y] = owner - 1
    acc[...] = jnp.zeros_like(acc)
    first, last = span_of[0], span_of[1]
    passes = lax.div(jnp.maximum(last - first + CHUNK, 0), CHUNK)
    step = 64

    def one_pass(j, carry):
        q = first + j * CHUNK

        def block(n, sums):
            sums = list(sums)
            start = pl.multiple_of(n * step, step)
            for t in range(step // 8):
                v = values[pl.ds(start + 8 * t, 8)]
                o = owners[pl.ds(start + 8 * t, 8)]
                for c in range(CHUNK):
                    sums[c] = sums[c] + jnp.where(o == q + c, v, 0.0)
            return tuple(sums)

        zero = jnp.zeros((8, depth), jnp.float32)
        sums = lax.fori_loop(0, values.shape[0] // step, block, (zero,) * CHUNK)
        for c in range(CHUNK):
            row = jnp.minimum(info[CONTROL] + q + c, acc.shape[0] - 1)
            inside = (q + c <= last).astype(jnp.float32)
            acc[pl.ds(row, 1)] = acc[pl.ds(row, 1)] + inside * jnp.sum(
                sums[c], axis=0, keepdims=True
            )
        return carry

    lax.fori_loop(0, passes, one_pass, 0)
    out[...] = lax.dot_general(
        jnp.ones((8, depth), jnp.float32),
        acc[...],
        (((1,), (1,)), ((), ())),
        precision=lax.Precision.HIGHEST,
        preferred_element_type=jnp.float32,
    )


def final_kernel(info, fixed, inner, ring, span_a, span_b, state, packed, out, lo, hi):
    count_x = state.shape[1]
    select_halos(info[SPAN_EVEN] == 1, span_a, span_b, lo, hi)

    def field(m, x):
        if x == 0 or x == count_x - 1:
            return fixed[0 if x == 0 else 1, m]
        return inner[m, x - 1]

    def beyond(end, came, m):
        fill = None
        if C[m][1] != 0:
            fill = (hi if C[m][1] == 1 else lo)[FACE, end : end + 1]
        return ring[end, came.index(m)], fill

    for x in range(count_x):
        result = advance_slab(
            field, lo, hi, state, packed, x, info,
            functools.partial(beyond, 0, XM), functools.partial(beyond, 1, XP),
        )
        for m in range(MEMBERS):
            out[m, x] = result[m]


def vmem():
    return pl.BlockSpec(memory_space=pltpu.VMEM)


def smem():
    return pl.BlockSpec(memory_space=pltpu.SMEM)


def f32(*shape):
    return jax.ShapeDtypeStruct(shape, jnp.float32)


def run(kernel, inputs, in_specs, outs, scratch=(), out_specs=None, limit=None):
    nbytes = sum(4 * e.size for e in inputs) + sum(4 * e.size for e in outs)
    return pl.pallas_call(
        kernel,
        out_shape=tuple(outs),
        in_specs=in_specs,
        out_specs=tuple(out_specs or [vmem()] * len(outs)),
        scratch_shapes=list(scratch),
        cost_estimate=pl.CostEstimate(
            flops=2 * nbytes, bytes_accessed=nbytes, transcendentals=0
        ),
        compiler_params=pltpu.CompilerParams(vmem_limit_bytes=limit),
    )(*inputs)


def swap_pairs(count, start, closed):
    pairs = []
    for i in range(start, count if closed else count - 1, 2):
        j = (i + 1) % count
        pairs += [(i, j), (j, i)]
    return pairs


def swap(parts, axis, closed):
    count = lax.axis_size(axis)
    assert count % 2 == 0
    return [
        lax.ppermute(part, axis, swap_pairs(count, start, closed))
        for start, part in enumerate(parts)
    ]


def shards(primal, adjoint, solid, links):
    members, count_x, count_y, depth = adjoint.shape
    assert members == MEMBERS and depth == 128 and count_y % 8 == 0
    stream_count, span_count = lax.axis_size("stream"), lax.axis_size("span")
    span, stream = lax.axis_index("span"), lax.axis_index("stream")
    share = PERIOD_PARTS * (count_y // (SEGMENT_WIDTH + 2)) * SEGMENT_CONTROLS
    controls = share * span_count
    assert share < (1 << BITS) - 1 and controls <= depth
    info = jnp.stack(
        [
            1 - span % 2,
            1 - stream % 2,
            jnp.where(span == 0, 0, -1),
            jnp.where(span == span_count - 1, count_y - 1, -1),
            span * share,
        ]
    ).astype(jnp.int32)
    row = (count_x, depth)
    halo = f32(FACE + 1, *row)
    halo_scratch = [pltpu.VMEM(halo.shape, jnp.float32)] * 2
    slab = (count_y, depth)

    span_a, span_b = swap(
        run(
            pack_span_kernel,
            [info, adjoint],
            [smem(), pl.BlockSpec(memory_space=pl.ANY)],
            [halo, halo],
            [pltpu.VMEM((FACE, *row), jnp.float32)] * 2 + [pltpu.SemaphoreType.DMA((2 * FACE,))],
        ),
        "span",
        False,
    )
    slots = -(-links.shape[2] // 128) * 128
    state, packed, span_of = run(
        prepare_kernel,
        [info, primal, solid, links],
        [smem(), vmem(), vmem(), vmem()],
        [
            f32(7, count_x, *slab),
            jax.ShapeDtypeStruct((GROUPS, count_x, *slab), jnp.int32),
            jax.ShapeDtypeStruct((2,), jnp.int32),
        ],
        [pltpu.VMEM((8, slots), jnp.int32)],
        [vmem(), vmem(), smem()],
    )
    message = f32(message_rows(count_y), depth)
    edge, *parts = run(
        edge_kernel,
        [info, adjoint, span_a, span_b, state, packed],
        [smem()] + [vmem()] * 5,
        [f32(2, MEMBERS, *slab), message, message],
        halo_scratch,
    )
    stream_a, stream_b = swap(parts, "stream", True)
    (inner,) = run(
        interior_kernel,
        [info, adjoint, span_a, span_b, state, packed],
        [smem()] + [vmem()] * 5,
        [f32(MEMBERS, count_x - 2, *slab)],
        halo_scratch,
    )
    fixed, ring, *parts = run(
        correct_kernel,
        [info, adjoint, span_a, span_b, stream_a, stream_b, state, packed, edge, inner],
        [smem()] + [vmem()] * 9,
        [f32(2, MEMBERS, *slab), f32(2, FACE, *slab), halo, halo],
        halo_scratch
        + [
            pltpu.VMEM((2, *message.shape), jnp.float32),
            pltpu.VMEM((2, *halo.shape), jnp.float32),
        ],
    )
    next_a, next_b = swap(parts, "span", False)
    (partial,) = run(
        sensitivity_kernel,
        [info, span_of, primal, state, packed, fixed, inner],
        [smem(), smem()] + [vmem()] * 5,
        [f32(8, depth)],
        [
            pltpu.VMEM((18 * count_x * count_y, depth), jnp.float32),
            pltpu.VMEM((18 * count_x * count_y, depth), jnp.int32),
            pltpu.VMEM((depth, depth), jnp.float32),
        ],
    )
    everyone = stream_count * span_count
    copies = jnp.broadcast_to(partial[:1], (everyone, depth))
    copies = lax.all_to_all(copies, ("stream", "span"), 0, 0, tiled=True)
    sensitivity = jnp.sum(copies, axis=0)[:controls] * (
        SENS_SCALE / (stream_count // PERIOD_PARTS)
    )
    (result,) = run(
        final_kernel,
        [info, fixed, inner, ring, next_a, next_b, state, packed],
        [smem()] + [vmem()] * 7,
        [f32(MEMBERS, count_x, *slab)],
        halo_scratch,
    )
    return result, sensitivity


def solution(mesh):
    placed = (
        P(None, "stream", "span", None),
        P(None, "stream", "span", None),
        P("stream", "span", None),
        P(None, "stream", "span"),
    )
    return jax.shard_map(
        shards,
        mesh=mesh,
        in_specs=placed,
        out_specs=(P(None, "stream", "span", None), P()),
        check_vma=False,
    )
```

time: 274 us -> 49.5 us (0.18)
  local copies, waits for them, and re-layouts: 185 us -> 3.82 us
  blocking collectives: 37.8 us -> 0 us
  Pallas kernels: 0 us -> 23.4 us
  other arithmetic: 23.6 us -> 0.54 us
    gather x6 -> x0, local copies, waits for them, and re-layouts: 88.7 us -> none  [the longest x2 38.5 us: shards(): heat_back = 1.0 - flattened[heat_source, safe_cells]]
    unnamed x71 -> x16, local copies, waits for them, and re-layouts: 67.5 us -> 1.87 us
    psum x1 -> x0, blocking collectives: 37.8 us -> none  [shards(): assembled = lax.psum(partial_value, ('stream', 'span'))]
    pallas_call x0 -> x7, Pallas kernels: none -> 23.4 us  [run(): pl.pallas_call(kernel, out_shape=tuple(outs), in_specs=in_specs, out_spec...]
    another operation x4 -> x1, local copies, waits for them, and re-layouts: 22.4 us -> 0.65 us  [shards(): jnp.stack([1 - span % 2, 1 - stream % 2, jnp.where(span == 0, 0, -1), jnp...]
    ppermute x8 -> x6, starting transfers between devices: 20 us -> 12.8 us  [swap(): lax.ppermute(part, axis, swap_pairs(count, start, closed))]
    all_to_all x0 -> x1, starting transfers between devices: none -> 5.53 us  [shards(): copies = lax.all_to_all(copies, ('stream', 'span'), 0, 0, tiled=True)]
    mul x11 -> x1, other arithmetic: 6.03 us -> 0.52 us  [shards(): jnp.sum(copies, axis=0)[:controls]]
  transfers between devices with their start and end apart: 8 -> 7, of which waited for: 3 -> 2; matrix products, arithmetic and copies ran while one was open for 27% -> 0% of each run, Pallas kernels for 0% -> 22%
where the time goes in v1:
time: 49.5 us; the launch traced here: 49.1 us
  Pallas kernels  23.4 us (47%)
  starting transfers between devices  18.3 us (37%)
  local copies, waits for them, and re-layouts  3.82 us (8%)
  waiting for transfers between devices  2.22 us (4%)
  between operations  0.77 us (2%)
  other arithmetic  0.54 us (1%)
    pallas_call x7, Pallas kernels, run(): pl.pallas_call(kernel, out_shape=tuple(outs), in_specs=in_specs, out_spec...  23.4 us
    ppermute x6, starting transfers between devices, swap(): lax.ppermute(part, axis, swap_pairs(count, start, closed))  12.8 us
    all_to_all x1, starting transfers between devices, shards(): copies = lax.all_to_all(copies, ('stream', 'span'), 0, 0, tiled=True)  5.53 us
    ppermute x6, waiting for transfers between devices, swap(): lax.ppermute(part, axis, swap_pairs(count, start, closed))  2.21 us
    unnamed x16, local copies, waits for them, and re-layouts  1.87 us
  transfers between devices with their start and end apart: 7, of which 2 were waited for; matrix products, arithmetic and copies ran while one was open for 0% of the time, Pallas kernels for 22%

profile of v1, /device:TPU:1, one launch (start us, length us, event | category | flops | bytes accessed | tf_op | source)
XLA Modules:
  0.0 49.1 jit_solution(4495947909701251298)
XLA Ops:
  0.7 0.7 %stack.23.info = s32[5]{0:T(128)} concatenate(s32[1]{0:T(128)} %bitcast, s32[1]{0:T(128)} %bitcast.1, s32[1]{0:T(128)} %bitcast.2, s32[1]{0:T(128)} %bitcast.3, s32[1]{0:T(128)} %bitcast.4), dimensions={0} | concatenate | bytes 40 | tf_op jit(solution)/shard_map/stack | solution.py:540
  1.3 2.2 %shard_map.59 = (f32[7,8,128]{2,1,0:T(8,128)}, f32[7,8,128]{2,1,0:T(8,128)}) custom-call(s32[5]{0:T(128)} %stack.23.info, f32[26,8,16,128]{3,2,1,0:T(8,128)} %adjoint.5), custom_call_target="tpu_custom_call" | custom-call | flops 3522600 | bytes 1761300 | tf_op jit(solution)/shard_map/pallas_call | solution.py:502
  3.5 0.1 collective-permute-start
  3.6 4.5 %collective-permute-start.1 = (f32[7,8,128]{2,1,0:T(8,128)}, f32[7,8,128]{2,1,0:T(8,128)S(1)}, u32[]{:S(2)}, u32[]{:S(2)}) collective-permute-start(f32[7,8,128]{2,1,0:T(8,128)} %get-tuple-element.15), channel_id=1, source_target_pairs={{1,2},{2,1},{5,6},{6,5},{9,10},{10,9},{13,14},{14,13},{17,18},{18,... | collective-permute-start | bytes 86024 | tf_op jit(solution)/shard_map/ppermute | solution.py:527
  8.1 3.5 %shard_map.60 = (f32[7,8,16,128]{3,2,1,0:T(8,128)}, s32[5,8,16,128]{3,2,1,0:T(8,128)}, s32[2]{0:T(128)}) custom-call(s32[5]{0:T(128)} %stack.23.info, f32[26,8,16,128]{3,2,1,0:T(8,128)} %primal.3, s32[8,16,128]{2,1,0:T(8,128)} %solid.1, s32[3,1,2464]{2,1,0:T(1,128)} %links.1), custom_call_target="tpu_custom_call" | custom-call | flops 5171000 | bytes 2585500 | tf_op jit(solution)/shard_map/pallas_call | solution.py:502
  11.6 0.0 collective-permute-done.recv_a.span_a
  11.7 0.0 copy-start
  11.7 0.0 collective-permute-done.1.recv_b.span_b
  11.7 0.0 copy-start.1
  11.7 0.6 %copy-done = f32[7,8,128]{2,1,0:T(8,128)} copy-done((f32[7,8,128]{2,1,0:T(8,128)}, f32[7,8,128]{2,1,0:T(8,128)S(1)}, u32[]{:S(2)}) %copy-start) | copy-done | bytes 28696
  12.3 0.0 copy-done.1
  12.3 2.8 %shard_map.61 = (f32[2,26,16,128]{3,2,1,0:T(8,128)}, f32[280,128]{1,0:T(8,128)}, f32[280,128]{1,0:T(8,128)}) custom-call(s32[5]{0:T(128)} %stack.23.info, f32[26,8,16,128]{3,2,1,0:T(8,128)} %adjoint.5, f32[7,8,128]{2,1,0:T(8,128)} %copy-done, f32[7,8,128]{2,1,0:T(8,128)} %copy-done.1, f32[7,8,16,128]{3,2,1,0:T(8,128)} %get-tuple-element.16.state, ...), custom_call_target="tpu_custom_call" | custom-call | flops 6520872 | bytes 3260436 | tf_op jit(solution)/shard_map/pallas_call | solution.py:502
  15.1 1.2 %collective-permute-start.2 = (f32[280,128]{1,0:T(8,128)}, f32[280,128]{1,0:T(8,128)S(1)}, u32[]{:S(2)}, u32[]{:S(2)}) collective-permute-start(f32[280,128]{1,0:T(8,128)} %get-tuple-element.18), channel_id=1, source_target_pairs={{0,4},{4,0},{8,12},{12,8},{16,20},{20,16},{24,28},{28,24},{1,5},{5... | collective-permute-start | bytes 430088 | tf_op jit(solution)/shard_map/ppermute | solution.py:527
  16.3 3.3 %collective-permute-start.3 = (f32[280,128]{1,0:T(8,128)}, f32[280,128]{1,0:T(8,128)S(1)}, u32[]{:S(2)}, u32[]{:S(2)}) collective-permute-start(f32[280,128]{1,0:T(8,128)} %get-tuple-element.19), channel_id=1, source_target_pairs={{4,8},{8,4},{12,16},{16,12},{20,24},{24,20},{28,0},{0,28},{5,9},{9... | collective-permute-start | bytes 430088 | tf_op jit(solution)/shard_map/ppermute | solution.py:527
  19.6 3.5 %shard_map.62.inner = f32[26,6,16,128]{3,2,1,0:T(8,128)} custom-call(s32[5]{0:T(128)} %stack.23.info, f32[26,8,16,128]{3,2,1,0:T(8,128)} %adjoint.5, f32[7,8,128]{2,1,0:T(8,128)} %copy-done, f32[7,8,128]{2,1,0:T(8,128)} %copy-done.1, f32[7,8,16,128]{3,2,1,0:T(8,128)} %get-tuple-element.16.state, s32[5,8,16,128]{3,2,1,0:T(8,128)} %get-tuple-element.17.packed), custom_call_target="tpu_custom_call" | custom-call | flops 7651368 | bytes 3825684 | tf_op jit(solution)/shard_map/pallas_call | solution.py:502
  23.1 0.0 collective-permute-done.2.recv_a
  23.1 0.0 copy-start.2
  23.1 0.1 collective-permute-done.3.recv_b
  23.2 0.0 copy-start.3
  23.2 0.5 %copy-done.2 = f32[280,128]{1,0:T(8,128)} copy-done((f32[280,128]{1,0:T(8,128)}, f32[280,128]{1,0:T(8,128)S(1)}, u32[]{:S(2)}) %copy-start.2) | copy-done | bytes 143384
  23.7 0.1 copy-done.3
  23.9 3.4 %shard_map.63 = (f32[2,26,16,128]{3,2,1,0:T(8,128)}, f32[2,6,16,128]{3,2,1,0:T(8,128)}, f32[7,8,128]{2,1,0:T(8,128)}, f32[7,8,128]{2,1,0:T(8,128)}) custom-call(s32[5]{0:T(128)} %stack.23.info, f32[26,8,16,128]{3,2,1,0:T(8,128)} %adjoint.5, f32[7,8,128]{2,1,0:T(8,128)} %copy-done, f32[7,8,128]{2,1,0:T(8,128)} %copy-done.1, f32[280,128]{1,0:T(8,128)} %copy-done.2, ...), custom_call_target="tpu_custom_call" | custom-call | flops 10240040 | bytes 5120020 | tf_op jit(solution)/shard_map/pallas_call | solution.py:502
  27.2 0.0 copy-start.7
  27.2 0.0 copy-start.6
  27.3 4.2 %shard_map.65 = f32[8,128]{1,0:T(8,128)} custom-call(s32[5]{0:T(128)} %stack.23.info, s32[2]{0:T(128)} %get-tuple-element.25.span_of, f32[26,8,16,128]{3,2,1,0:T(8,128)} %primal.3, f32[7,8,16,128]{3,2,1,0:T(8,128)} %get-tuple-element.16.state, s32[5,8,16,128]{3,2,1,0:T(8,128)} %get-tuple-element.17.packed, f32[2,26,16,128]{3,2,1,0:T(8,128)} %get-tuple-element.21.fixed, ...), custom_call_target="tpu_custom_call" | custom-call | flops 8396856 | bytes 4198428 | tf_op jit(solution)/shard_map/pallas_call | solution.py:502
  31.5 0.7 %slice_bitcast_fusion = f32[128]{0:T(128)S(1)} fusion(f32[8,128]{1,0:T(8,128)} %shard_map.65), kind=kLoop, calls=%fused_computation | loop fusion | bytes 1024 | tf_op jit(solution)/shard_map/slice | solution.py:618
  32.1 0.6 %broadcast_in_dim.2 = f32[32,1,128]{2,1,0:T(1,128)} broadcast(f32[128]{0:T(128)S(1)} %slice_bitcast_fusion), dimensions={2} | broadcast | bytes 16896 | tf_op jit(solution)/shard_map/broadcast_in_dim | solution.py:618
  32.8 5.5 %all-to-all-start = ((f32[32,1,128]{2,1,0:T(1,128)}), f32[32,1,128]{2,1,0:T(1,128)S(1)}, u32[]{:S(2)}, u32[]{:S(2)}) async-start(f32[32,1,128]{2,1,0:T(1,128)} %broadcast_in_dim.2), calls=%async_computation | async-start | bytes 32768 | tf_op jit(solution)/shard_map/all_to_all | solution.py:619
  38.3 0.0 copy-done.7
  38.3 0.3 collective-permute-start.4
  38.6 0.0 copy-done.6
  38.6 3.4 %collective-permute-start.5 = (f32[7,8,128]{2,1,0:T(8,128)S(1)}, f32[7,8,128]{2,1,0:T(8,128)S(1)}, u32[]{:S(2)}, u32[]{:S(2)}) collective-permute-start(f32[7,8,128]{2,1,0:T(8,128)S(1)} %copy-done.6), channel_id=1, source_target_pairs={{1,2},{2,1},{5,6},{6,5},{9,10},{10,9},{13,14},{14,13},{17,18},{18,... | collective-permute-start | bytes 86024 | tf_op jit(solution)/shard_map/ppermute | solution.py:527
  42.0 0.0 collective-permute-done.4.span_a
  42.0 0.0 copy-start.4
  42.0 2.1 %collective-permute-done.5.span_b = f32[7,8,128]{2,1,0:T(8,128)S(1)} collective-permute-done((f32[7,8,128]{2,1,0:T(8,128)S(1)}, f32[7,8,128]{2,1,0:T(8,128)S(1)}, u32[]{:S(2)}, u32[]{:S(2)}) %collective-permute-start.5) | collective-permute-done | bytes 28704 | tf_op jit(solution)/shard_map/ppermute | solution.py:527
  44.1 0.0 copy-start.5
  44.1 0.0 copy-done.4
  44.1 0.6 %copy-done.5 = f32[7,8,128]{2,1,0:T(8,128)} copy-done((f32[7,8,128]{2,1,0:T(8,128)}, f32[7,8,128]{2,1,0:T(8,128)S(1)}, u32[]{:S(2)}) %copy-start.5) | copy-done | bytes 28696
  44.7 3.8 %shard_map.64 = f32[26,8,16,128]{3,2,1,0:T(8,128)} custom-call(s32[5]{0:T(128)} %stack.23.info, f32[2,26,16,128]{3,2,1,0:T(8,128)} %get-tuple-element.21.fixed, f32[26,6,16,128]{3,2,1,0:T(8,128)} %shard_map.62.inner, f32[2,6,16,128]{3,2,1,0:T(8,128)} %get-tuple-element.22.ring, f32[7,8,128]{2,1,0:T(8,128)} %copy-done.4, f32[7,8,128]{2,1,0:T(8,128)} %copy-done.5, ...), custom_call_target="tpu_custom_call" | custom-call | flops 8699944 | bytes 4349972 | tf_op jit(solution)/shard_map/pallas_call | solution.py:502
  48.6 0.0 all-to-all-done
  48.6 0.5 %broadcast_multiply_fusion = f32[128]{0:T(128)} fusion(f32[128]{0:T(128)S(1)} %reduce_sum.9), kind=kLoop, calls=%fused_computation.1 | loop fusion | flops 128 | bytes 1024 | tf_op jit(solution)/shard_map/mul | solution.py:620
  (1 shorter events, 0.0 us)
Async XLA Ops:
  3.5 8.1 %collective-permute-start = (f32[7,8,128]{2,1,0:T(8,128)}, f32[7,8,128]{2,1,0:T(8,128)S(1)}, u32[]{:S(2)}, u32[]{:S(2)}) collective-permute-start(f32[7,8,128]{2,1,0:T(8,128)} %get-tuple-element.14), channel_id=1, source_target_pairs={{0,1},{1,0},{2,3},{3,2},{4,5},{5,4},{6,7},{7,6},{8,9},{9,8},{10,11... | collective-permute-start | bytes 86024 | tf_op jit(solution)/shard_map/ppermute | solution.py:527
  3.6 8.1 %collective-permute-start.1 = (f32[7,8,128]{2,1,0:T(8,128)}, f32[7,8,128]{2,1,0:T(8,128)S(1)}, u32[]{:S(2)}, u32[]{:S(2)}) collective-permute-start(f32[7,8,128]{2,1,0:T(8,128)} %get-tuple-element.15), channel_id=1, source_target_pairs={{1,2},{2,1},{5,6},{6,5},{9,10},{10,9},{13,14},{14,13},{17,18},{18,... | collective-permute-start | bytes 86024 | tf_op jit(solution)/shard_map/ppermute | solution.py:527
  11.7 0.6 %copy-start = (f32[7,8,128]{2,1,0:T(8,128)}, f32[7,8,128]{2,1,0:T(8,128)S(1)}, u32[]{:S(2)}) copy-start(f32[7,8,128]{2,1,0:T(8,128)S(1)} %collective-permute-done.recv_a.span_a) | copy-start | bytes 86020
  11.7 0.6 %copy-start.1 = (f32[7,8,128]{2,1,0:T(8,128)}, f32[7,8,128]{2,1,0:T(8,128)S(1)}, u32[]{:S(2)}) copy-start(f32[7,8,128]{2,1,0:T(8,128)S(1)} %collective-permute-done.1.recv_b.span_b) | copy-start | bytes 86020
  15.1 8.0 %collective-permute-start.2 = (f32[280,128]{1,0:T(8,128)}, f32[280,128]{1,0:T(8,128)S(1)}, u32[]{:S(2)}, u32[]{:S(2)}) collective-permute-start(f32[280,128]{1,0:T(8,128)} %get-tuple-element.18), channel_id=1, source_target_pairs={{0,4},{4,0},{8,12},{12,8},{16,20},{20,16},{24,28},{28,24},{1,5},{5... | collective-permute-start | bytes 430088 | tf_op jit(solution)/shard_map/ppermute | solution.py:527
  16.3 6.9 %collective-permute-start.3 = (f32[280,128]{1,0:T(8,128)}, f32[280,128]{1,0:T(8,128)S(1)}, u32[]{:S(2)}, u32[]{:S(2)}) collective-permute-start(f32[280,128]{1,0:T(8,128)} %get-tuple-element.19), channel_id=1, source_target_pairs={{4,8},{8,4},{12,16},{16,12},{20,24},{24,20},{28,0},{0,28},{5,9},{9... | collective-permute-start | bytes 430088 | tf_op jit(solution)/shard_map/ppermute | solution.py:527
  23.1 0.7 %copy-start.2 = (f32[280,128]{1,0:T(8,128)}, f32[280,128]{1,0:T(8,128)S(1)}, u32[]{:S(2)}) copy-start(f32[280,128]{1,0:T(8,128)S(1)} %collective-permute-done.2.recv_a) | copy-start | bytes 430084
  23.2 0.7 %copy-start.3 = (f32[280,128]{1,0:T(8,128)}, f32[280,128]{1,0:T(8,128)S(1)}, u32[]{:S(2)}) copy-start(f32[280,128]{1,0:T(8,128)S(1)} %collective-permute-done.3.recv_b) | copy-start | bytes 430084
  27.2 11.1 %copy-start.7 = (f32[7,8,128]{2,1,0:T(8,128)S(1)}, f32[7,8,128]{2,1,0:T(8,128)}, u32[]{:S(2)}) copy-start(f32[7,8,128]{2,1,0:T(8,128)} %get-tuple-element.23) | copy-start | bytes 86020
  27.2 11.4 %copy-start.6 = (f32[7,8,128]{2,1,0:T(8,128)S(1)}, f32[7,8,128]{2,1,0:T(8,128)}, u32[]{:S(2)}) copy-start(f32[7,8,128]{2,1,0:T(8,128)} %get-tuple-element.24) | copy-start | bytes 86020
  32.8 15.8 %all-to-all-start = ((f32[32,1,128]{2,1,0:T(1,128)}), f32[32,1,128]{2,1,0:T(1,128)S(1)}, u32[]{:S(2)}, u32[]{:S(2)}) async-start(f32[32,1,128]{2,1,0:T(1,128)} %broadcast_in_dim.2), calls=%async_computation | async-start | bytes 32768 | tf_op jit(solution)/shard_map/all_to_all | solution.py:619
  38.3 3.7 %collective-permute-start.4 = (f32[7,8,128]{2,1,0:T(8,128)S(1)}, f32[7,8,128]{2,1,0:T(8,128)S(1)}, u32[]{:S(2)}, u32[]{:S(2)}) collective-permute-start(f32[7,8,128]{2,1,0:T(8,128)S(1)} %copy-done.7), channel_id=1, source_target_pairs={{0,1},{1,0},{2,3},{3,2},{4,5},{5,4},{6,7},{7,6},{8,9},{9,8},{10,11... | collective-permute-start | bytes 86024 | tf_op jit(solution)/shard_map/ppermute | solution.py:527
  38.6 5.5 %collective-permute-start.5 = (f32[7,8,128]{2,1,0:T(8,128)S(1)}, f32[7,8,128]{2,1,0:T(8,128)S(1)}, u32[]{:S(2)}, u32[]{:S(2)}) collective-permute-start(f32[7,8,128]{2,1,0:T(8,128)S(1)} %copy-done.6), channel_id=1, source_target_pairs={{1,2},{2,1},{5,6},{6,5},{9,10},{10,9},{13,14},{14,13},{17,18},{18,... | collective-permute-start | bytes 86024 | tf_op jit(solution)/shard_map/ppermute | solution.py:527
  42.0 2.1 %copy-start.4 = (f32[7,8,128]{2,1,0:T(8,128)}, f32[7,8,128]{2,1,0:T(8,128)S(1)}, u32[]{:S(2)}) copy-start(f32[7,8,128]{2,1,0:T(8,128)S(1)} %collective-permute-done.4.span_a) | copy-start | bytes 86020
  44.1 0.6 %copy-start.5 = (f32[7,8,128]{2,1,0:T(8,128)}, f32[7,8,128]{2,1,0:T(8,128)S(1)}, u32[]{:S(2)}) copy-start(f32[7,8,128]{2,1,0:T(8,128)S(1)} %collective-permute-done.5.span_b) | copy-start | bytes 86020

commit v2 on v1

--- a/solution.py
+++ b/solution.py
@@ -178,7 +178,24 @@
 SPAN_EVEN, STREAM_EVEN, Y_FIRST, Y_LAST, CONTROL = range(5)
 
 
-def pack_span_kernel(info, field, out_a, out_b, lo, hi, sems):
+def position(count_y):
+    span, stream = lax.axis_index("span"), lax.axis_index("stream")
+    at_end = span == lax.axis_size("span") - 1
+    return (
+        lax.rem(span, 2) == 0,
+        lax.rem(stream, 2) == 0,
+        jnp.where(span == 0, 0, -1),
+        jnp.where(at_end, count_y - 1, -1),
+        span * control_share(count_y),
+    )
+
+
+def control_share(count_y):
+    return PERIOD_PARTS * (count_y // (SEGMENT_WIDTH + 2)) * SEGMENT_CONTROLS
+
+
+def pack_span_kernel(field, out_a, out_b, lo, hi, sems):
+    info = position(field.shape[2])
     rows = field.shape[2]
     copies = []
     for k in range(FACE):
@@ -190,7 +207,7 @@
         copy.start()
     for copy in copies:
         copy.wait()
-    even = info[SPAN_EVEN] == 1
+    even = info[SPAN_EVEN]
     for k in range(FACE):
         out_a[k] = pick(even, hi[k], lo[k])
         out_b[k] = pick(even, lo[k], hi[k])
@@ -198,8 +215,9 @@
     out_b[FACE] = jnp.zeros_like(out_b[FACE])
 
 
-def prepare_kernel(info, primal, solid, links, state, packed, span_of, slots):
+def prepare_kernel(primal, solid, links, state, packed, span_of, slots):
     count_x, count_y, depth = solid.shape
+    info = position(count_y)
     cells = count_x * count_y * depth
     for x in range(count_x):
         f = [primal[m, x] for m in range(MEMBERS)]
@@ -287,11 +305,12 @@
     lo[...] = pick(even, recv_b[...], recv_a[...])
 
 
-def edge_kernel(info, adjoint, recv_a, recv_b, state, packed, edge, out_a, out_b, lo, hi):
+def edge_kernel(adjoint, recv_a, recv_b, state, packed, edge, out_a, out_b, lo, hi):
     count_x, count_y = state.shape[1:3]
-    select_halos(info[SPAN_EVEN] == 1, recv_a, recv_b, lo, hi)
+    info = position(count_y)
+    select_halos(info[SPAN_EVEN], recv_a, recv_b, lo, hi)
     field = lambda m, x: adjoint[m, x]
-    even = info[STREAM_EVEN] == 1
+    even = info[STREAM_EVEN]
     for side, x, sent, flagged in ((0, 0, XP, XM), (1, count_x - 1, XM, XP)):
         out = advance_slab(field, lo, hi, state, packed, x, info)
         for m in range(MEMBERS):
@@ -323,9 +342,10 @@
             write(out_b)
 
 
-def interior_kernel(info, adjoint, recv_a, recv_b, state, packed, inner, lo, hi):
+def interior_kernel(adjoint, recv_a, recv_b, state, packed, inner, lo, hi):
     count_x = state.shape[1]
-    select_halos(info[SPAN_EVEN] == 1, recv_a, recv_b, lo, hi)
+    info = position(state.shape[2])
+    select_halos(info[SPAN_EVEN], recv_a, recv_b, lo, hi)
     field = lambda m, x: adjoint[m, x]
     for x in range(1, count_x - 1):
         out = advance_slab(field, lo, hi, state, packed, x, info)
@@ -334,12 +354,13 @@
 
 
 def correct_kernel(
-    info, adjoint, span_a, span_b, recv_a, recv_b, state, packed, edge, inner,
+    adjoint, span_a, span_b, recv_a, recv_b, state, packed, edge, inner,
     fixed, ring, out_a, out_b, lo, hi, message, send,
 ):
     count_x, count_y = state.shape[1:3]
-    select_halos(info[SPAN_EVEN] == 1, span_a, span_b, lo, hi)
-    even = info[STREAM_EVEN] == 1
+    info = position(count_y)
+    select_halos(info[SPAN_EVEN], span_a, span_b, lo, hi)
+    even = info[STREAM_EVEN]
     message[1] = pick(even, recv_a[...], recv_b[...])
     message[0] = pick(even, recv_b[...], recv_a[...])
     rows, lanes = indices(state.shape[2:])
@@ -388,7 +409,7 @@
         for end, came in ((0, XM), (1, XP)):
             m = [e for e in came if e in group][0]
             send[side, FACE, end : end + 1] = ring[end, came.index(m), row : row + 1]
-    span_even = info[SPAN_EVEN] == 1
+    span_even = info[SPAN_EVEN]
     out_a[...] = pick(span_even, send[1], send[0])
     out_b[...] = pick(span_even, send[0], send[1])
 
@@ -396,8 +417,9 @@
 CHUNK = 4
 
 
-def sensitivity_kernel(info, span_of, primal, state, packed, fixed, inner, out, values, owners, acc):
+def sensitivity_kernel(span_of, primal, state, packed, fixed, inner, out, values, owners, acc):
     count_x, count_y, depth = state.shape[1:]
+    info = position(count_y)
 
     def field(m, x):
         if x == 0 or x == count_x - 1:
@@ -452,18 +474,26 @@
         return carry
 
     lax.fori_loop(0, passes, one_pass, 0)
-    out[...] = lax.dot_general(
+    total = lax.dot_general(
         jnp.ones((8, depth), jnp.float32),
         acc[...],
         (((1,), (1,)), ((), ())),
         precision=lax.Precision.HIGHEST,
         preferred_element_type=jnp.float32,
     )
-
-
-def final_kernel(info, fixed, inner, ring, span_a, span_b, state, packed, out, lo, hi):
+    out[...] = jnp.broadcast_to(total[:1], out.shape[::2])[:, None, :]
+
+
+def total_kernel(copies, out):
+    periods = lax.axis_size("stream") // PERIOD_PARTS
+    total = jnp.sum(copies[...], axis=0) * (SENS_SCALE / periods)
+    out[...] = total[:, : out.shape[1]]
+
+
+def final_kernel(fixed, inner, ring, span_a, span_b, state, packed, out, lo, hi):
     count_x = state.shape[1]
-    select_halos(info[SPAN_EVEN] == 1, span_a, span_b, lo, hi)
+    info = position(state.shape[2])
+    select_halos(info[SPAN_EVEN], span_a, span_b, lo, hi)
 
     def field(m, x):
         if x == 0 or x == count_x - 1:
@@ -497,7 +527,7 @@
     return jax.ShapeDtypeStruct(shape, jnp.float32)
 
 
-def run(kernel, inputs, in_specs, outs, scratch=(), out_specs=None, limit=None):
+def run(kernel, inputs, in_specs, outs, scratch=(), out_specs=None, limit=12 << 20):
     nbytes = sum(4 * e.size for e in inputs) + sum(4 * e.size for e in outs)
     return pl.pallas_call(
         kernel,
@@ -533,19 +563,8 @@
     members, count_x, count_y, depth = adjoint.shape
     assert members == MEMBERS and depth == 128 and count_y % 8 == 0
     stream_count, span_count = lax.axis_size("stream"), lax.axis_size("span")
-    span, stream = lax.axis_index("span"), lax.axis_index("stream")
-    share = PERIOD_PARTS * (count_y // (SEGMENT_WIDTH + 2)) * SEGMENT_CONTROLS
-    controls = share * span_count
-    assert share < (1 << BITS) - 1 and controls <= depth
-    info = jnp.stack(
-        [
-            1 - span % 2,
-            1 - stream % 2,
-            jnp.where(span == 0, 0, -1),
-            jnp.where(span == span_count - 1, count_y - 1, -1),
-            span * share,
-        ]
-    ).astype(jnp.int32)
+    controls = control_share(count_y) * span_count
+    assert control_share(count_y) < (1 << BITS) - 1 and controls <= depth
     row = (count_x, depth)
     halo = f32(FACE + 1, *row)
     halo_scratch = [pltpu.VMEM(halo.shape, jnp.float32)] * 2
@@ -554,8 +573,8 @@
     span_a, span_b = swap(
         run(
             pack_span_kernel,
-            [info, adjoint],
-            [smem(), pl.BlockSpec(memory_space=pl.ANY)],
+            [adjoint],
+            [pl.BlockSpec(memory_space=pl.ANY)],
             [halo, halo],
             [pltpu.VMEM((FACE, *row), jnp.float32)] * 2 + [pltpu.SemaphoreType.DMA((2 * FACE,))],
         ),
@@ -565,8 +584,8 @@
     slots = -(-links.shape[2] // 128) * 128
     state, packed, span_of = run(
         prepare_kernel,
-        [info, primal, solid, links],
-        [smem(), vmem(), vmem(), vmem()],
+        [primal, solid, links],
+        [vmem()] * 3,
         [
             f32(7, count_x, *slab),
             jax.ShapeDtypeStruct((GROUPS, count_x, *slab), jnp.int32),
@@ -578,23 +597,23 @@
     message = f32(message_rows(count_y), depth)
     edge, *parts = run(
         edge_kernel,
-        [info, adjoint, span_a, span_b, state, packed],
-        [smem()] + [vmem()] * 5,
+        [adjoint, span_a, span_b, state, packed],
+        [vmem()] * 5,
         [f32(2, MEMBERS, *slab), message, message],
         halo_scratch,
     )
     stream_a, stream_b = swap(parts, "stream", True)
     (inner,) = run(
         interior_kernel,
-        [info, adjoint, span_a, span_b, state, packed],
-        [smem()] + [vmem()] * 5,
+        [adjoint, span_a, span_b, state, packed],
+        [vmem()] * 5,
         [f32(MEMBERS, count_x - 2, *slab)],
         halo_scratch,
     )
     fixed, ring, *parts = run(
         correct_kernel,
-        [info, adjoint, span_a, span_b, stream_a, stream_b, state, packed, edge, inner],
-        [smem()] + [vmem()] * 9,
+        [adjoint, span_a, span_b, stream_a, stream_b, state, packed, edge, inner],
+        [vmem()] * 9,
         [f32(2, MEMBERS, *slab), f32(2, FACE, *slab), halo, halo],
         halo_scratch
         + [
@@ -605,29 +624,25 @@
     next_a, next_b = swap(parts, "span", False)
     (partial,) = run(
         sensitivity_kernel,
-        [info, span_of, primal, state, packed, fixed, inner],
-        [smem(), smem()] + [vmem()] * 5,
-        [f32(8, depth)],
+        [span_of, primal, state, packed, fixed, inner],
+        [smem()] + [vmem()] * 5,
+        [f32(stream_count * span_count, 1, depth)],
         [
             pltpu.VMEM((18 * count_x * count_y, depth), jnp.float32),
             pltpu.VMEM((18 * count_x * count_y, depth), jnp.int32),
             pltpu.VMEM((depth, depth), jnp.float32),
         ],
     )
-    everyone = stream_count * span_count
-    copies = jnp.broadcast_to(partial[:1], (everyone, depth))
-    copies = lax.all_to_all(copies, ("stream", "span"), 0, 0, tiled=True)
-    sensitivity = jnp.sum(copies, axis=0)[:controls] * (
-        SENS_SCALE / (stream_count // PERIOD_PARTS)
-    )
+    copies = lax.all_to_all(partial, ("stream", "span"), 0, 0, tiled=True)
+    (sensitivity,) = run(total_kernel, [copies], [vmem()], [f32(1, controls)])
     (result,) = run(
         final_kernel,
-        [info, fixed, inner, ring, next_a, next_b, state, packed],
-        [smem()] + [vmem()] * 7,
+        [fixed, inner, ring, next_a, next_b, state, packed],
+        [vmem()] * 7,
         [f32(MEMBERS, count_x, *slab)],
         halo_scratch,
     )
-    return result, sensitivity
+    return result, sensitivity.reshape(controls)
 
 
 def solution(mesh):

time: 49.5 us -> 36.8 us (0.74)
  Pallas kernels: 23.4 us -> 8.42 us
  waiting for transfers between devices: 2.22 us -> 4.7 us
  local copies, waits for them, and re-layouts: 3.82 us -> 4.49 us
  other arithmetic: 0.54 us -> 0 us
    pallas_call x7 -> x8, Pallas kernels: 23.4 us -> 8.42 us  [run(): pl.pallas_call(kernel, out_shape=tuple(outs), in_specs=in_specs, out_spec...]
    unnamed x16 -> x10, local copies, waits for them, and re-layouts: 1.87 us -> 4.49 us
    ppermute x6, waiting for transfers between devices: 2.21 us -> 4.7 us  [swap(): lax.ppermute(part, axis, swap_pairs(count, start, closed))]
    slice x1 -> x0, local copies, waits for them, and re-layouts: 0.69 us -> none  [shards(): copies = jnp.broadcast_to(partial[:1], (everyone, depth))]
    another operation x1 -> x0, local copies, waits for them, and re-layouts: 0.65 us -> none  [shards(): jnp.stack([1 - span % 2, 1 - stream % 2, jnp.where(span == 0, 0, -1), jnp...]
    broadcast_in_dim x1 -> x0, local copies, waits for them, and re-layouts: 0.61 us -> none  [shards(): copies = jnp.broadcast_to(partial[:1], (everyone, depth))]
    mul x1 -> x0, other arithmetic: 0.52 us -> none  [shards(): jnp.sum(copies, axis=0)[:controls]]
  transfers between devices with their start and end apart: 7 -> 7, of which waited for: 2 -> 3; matrix products, arithmetic and copies ran while one was open for 0% -> 0% of each run, Pallas kernels for 22% -> 13%
where the time goes in v2:
time: 36.8 us
  starting transfers between devices  18.4 us (50%)
  Pallas kernels  8.42 us (23%)
  waiting for transfers between devices  4.7 us (13%)
  local copies, waits for them, and re-layouts  4.49 us (12%)
  between operations  0.74 us (2%)
    ppermute x6, starting transfers between devices, swap(): lax.ppermute(part, axis, swap_pairs(count, start, closed))  13 us
    pallas_call x8, Pallas kernels, run(): pl.pallas_call(kernel, out_shape=tuple(outs), in_specs=in_specs, out_spec...  8.42 us
    all_to_all x1, starting transfers between devices, shards(): copies = lax.all_to_all(partial, ('stream', 'span'), 0, 0, tiled=True)  5.4 us
    ppermute x6, waiting for transfers between devices, swap(): lax.ppermute(part, axis, swap_pairs(count, start, closed))  4.7 us
    unnamed x10, local copies, waits for them, and re-layouts  4.49 us
  transfers between devices with their start and end apart: 7, of which 3 were waited for; matrix products, arithmetic and copies ran while one was open for 0% of the time, Pallas kernels for 13%

profile of v2, /device:TPU:1, one launch (start us, length us, event | category | flops | bytes accessed | tf_op | source)
XLA Modules:
  0.0 36.8 jit_solution(14769473285601116408)
XLA Ops:
  0.6 0.0 copy-start
  0.6 1.4 %copy-done = f32[26,8,16,128]{3,2,1,0:T(8,128)S(1)} copy-done((f32[26,8,16,128]{3,2,1,0:T(8,128)S(1)}, f32[26,8,16,128]{3,2,1,0:T(8,128)}, u32[]{:S(2)}) %copy-start) | copy-done | bytes 1703960
  2.1 0.0 copy-start.1
  2.1 0.2 shard_map.59
  2.3 0.1 collective-permute-start
  2.3 4.6 %collective-permute-start.1 = (f32[7,8,128]{2,1,0:T(8,128)S(1)}, f32[7,8,128]{2,1,0:T(8,128)S(1)}, u32[]{:S(2)}, u32[]{:S(2)}) collective-permute-start(f32[7,8,128]{2,1,0:T(8,128)S(1)} %get-tuple-element.15), channel_id=1, source_target_pairs={{1,2},{2,1},{5,6},{6,5},{9,10},{10,9},{13,14},{14,13},{17,18},{18,... | collective-permute-start | bytes 86024 | tf_op jit(solution)/shard_map/ppermute | solution.py:557
  7.0 0.0 copy-start.2
  7.0 1.4 %copy-done.2 = f32[26,8,16,128]{3,2,1,0:T(8,128)S(1)} copy-done((f32[26,8,16,128]{3,2,1,0:T(8,128)S(1)}, f32[26,8,16,128]{3,2,1,0:T(8,128)}, u32[]{:S(2)}) %copy-start.2) | copy-done | bytes 1703960
  8.4 0.0 copy-start.3
  8.4 0.8 %copy-done.3 = s32[8,16,128]{2,1,0:T(8,128)S(1)} copy-done((s32[8,16,128]{2,1,0:T(8,128)S(1)}, s32[8,16,128]{2,1,0:T(8,128)}, u32[]{:S(2)}) %copy-start.3) | copy-done | bytes 65560
  9.3 0.0 copy-start.4
  9.3 0.8 %copy-done.4 = s32[3,1,2464]{2,1,0:T(1,128)S(1)} copy-done((s32[3,1,2464]{2,1,0:T(1,128)S(1)}, s32[3,1,2464]{2,1,0:T(1,128)}, u32[]{:S(2)}) %copy-start.4) | copy-done | bytes 29592
  10.0 1.7 %shard_map.60 = (f32[7,8,16,128]{3,2,1,0:T(8,128)S(1)}, s32[5,8,16,128]{3,2,1,0:T(8,128)S(1)}, s32[2]{0:T(128)S(1)}) custom-call(f32[26,8,16,128]{3,2,1,0:T(8,128)S(1)} %copy-done.2, s32[8,16,128]{2,1,0:T(8,128)S(1)} %copy-done.3, s32[3,1,2464]{2,1,0:T(1,128)S(1)} %copy-done.4), custom_call_target="tpu_custom_call" | custom-call | flops 5170960 | bytes 2585480 | tf_op jit(solution)/shard_map/pallas_call | solution.py:532
  11.7 0.0 collective-permute-done.recv_a.span_a
  11.7 0.0 collective-permute-done.1.recv_b.span_b
  11.7 0.0 copy-done.1
  11.8 0.3 shard_map.61
  12.1 1.3 %collective-permute-start.2 = (f32[280,128]{1,0:T(8,128)S(1)}, f32[280,128]{1,0:T(8,128)S(1)}, u32[]{:S(2)}, u32[]{:S(2)}) collective-permute-start(f32[280,128]{1,0:T(8,128)S(1)} %get-tuple-element.18), channel_id=1, source_target_pairs={{0,4},{4,0},{8,12},{12,8},{16,20},{20,16},{24,28},{28,24},{1,5},{5... | collective-permute-start | bytes 430088 | tf_op jit(solution)/shard_map/ppermute | solution.py:557
  13.4 3.3 %collective-permute-start.3 = (f32[280,128]{1,0:T(8,128)S(1)}, f32[280,128]{1,0:T(8,128)S(1)}, u32[]{:S(2)}, u32[]{:S(2)}) collective-permute-start(f32[280,128]{1,0:T(8,128)S(1)} %get-tuple-element.19), channel_id=1, source_target_pairs={{4,8},{8,4},{12,16},{16,12},{20,24},{24,20},{28,0},{0,28},{5,9},{9... | collective-permute-start | bytes 430088 | tf_op jit(solution)/shard_map/ppermute | solution.py:557
  16.7 0.8 %shard_map.62.inner = f32[26,6,16,128]{3,2,1,0:T(8,128)S(1)} custom-call(f32[26,8,16,128]{3,2,1,0:T(8,128)S(1)} %copy-done.1, f32[7,8,128]{2,1,0:T(8,128)S(1)} %collective-permute-done.recv_a.span_a, f32[7,8,128]{2,1,0:T(8,128)S(1)} %collective-permute-done.1.recv_b.span_b, f32[7,8,16,128]{3,2,1,0:T(8,128)S(1)} %get-tuple-element.16.state, ...), custom_call_target="tpu_custom_call" | custom-call | flops 7651328 | bytes 3825664 | tf_op jit(solution)/shard_map/pallas_call | solution.py:532
  17.4 0.7 %collective-permute-done.2.recv_a = f32[280,128]{1,0:T(8,128)S(1)} collective-permute-done((f32[280,128]{1,0:T(8,128)S(1)}, f32[280,128]{1,0:T(8,128)S(1)}, u32[]{:S(2)}, u32[]{:S(2)}) %collective-permute-start.2) | collective-permute-done | bytes 143392 | tf_op jit(solution)/shard_map/ppermute | solution.py:557
  18.1 1.9 %collective-permute-done.3.recv_b = f32[280,128]{1,0:T(8,128)S(1)} collective-permute-done((f32[280,128]{1,0:T(8,128)S(1)}, f32[280,128]{1,0:T(8,128)S(1)}, u32[]{:S(2)}, u32[]{:S(2)}) %collective-permute-start.3) | collective-permute-done | bytes 143392 | tf_op jit(solution)/shard_map/ppermute | solution.py:557
  20.0 0.2 shard_map.63
  20.3 2.5 %shard_map.65 = f32[32,1,128]{2,1,0:T(1,128)} custom-call(s32[2]{0:T(128)S(1)} %get-tuple-element.25.span_of, f32[26,8,16,128]{3,2,1,0:T(8,128)S(1)} %copy-done.2, f32[7,8,16,128]{3,2,1,0:T(8,128)S(1)} %get-tuple-element.16.state, s32[5,8,16,128]{3,2,1,0:T(8,128)S(1)} %get-tuple-element.17.packed, f32[2,26,16,128]{3,2,1,0:T(8,128)S(1)} %get-tuple-element.21.fixed, ...), custom_call_target="tpu_custom_call" | custom-call | flops 8421392 | bytes 4210696 | tf_op jit(solution)/shard_map/pallas_call | solution.py:532
  22.8 5.4 %all-to-all-start = ((f32[32,1,128]{2,1,0:T(1,128)}), f32[32,1,128]{2,1,0:T(1,128)S(1)}, u32[]{:S(2)}, u32[]{:S(2)}) async-start(f32[32,1,128]{2,1,0:T(1,128)} %shard_map.65), calls=%async_computation | async-start | bytes 32768 | tf_op jit(solution)/shard_map/all_to_all | solution.py:636
  28.2 0.3 collective-permute-start.4
  28.5 3.4 %collective-permute-start.5 = (f32[7,8,128]{2,1,0:T(8,128)S(1)}, f32[7,8,128]{2,1,0:T(8,128)S(1)}, u32[]{:S(2)}, u32[]{:S(2)}) collective-permute-start(f32[7,8,128]{2,1,0:T(8,128)S(1)} %get-tuple-element.24), channel_id=1, source_target_pairs={{1,2},{2,1},{5,6},{6,5},{9,10},{10,9},{13,14},{14,13},{17,18},{18,... | collective-permute-start | bytes 86024 | tf_op jit(solution)/shard_map/ppermute | solution.py:557
  31.9 0.0 collective-permute-done.4.span_a
  31.9 2.1 %collective-permute-done.5.span_b = f32[7,8,128]{2,1,0:T(8,128)S(1)} collective-permute-done((f32[7,8,128]{2,1,0:T(8,128)S(1)}, f32[7,8,128]{2,1,0:T(8,128)S(1)}, u32[]{:S(2)}, u32[]{:S(2)}) %collective-permute-start.5) | collective-permute-done | bytes 28704 | tf_op jit(solution)/shard_map/ppermute | solution.py:557
  34.0 2.2 %shard_map.64 = f32[26,8,16,128]{3,2,1,0:T(8,128)} custom-call(f32[2,26,16,128]{3,2,1,0:T(8,128)S(1)} %get-tuple-element.21.fixed, f32[26,6,16,128]{3,2,1,0:T(8,128)S(1)} %shard_map.62.inner, f32[2,6,16,128]{3,2,1,0:T(8,128)S(1)} %get-tuple-element.22.ring, f32[7,8,128]{2,1,0:T(8,128)S(1)} %collective-permute-done.4.span_a, ...), custom_call_target="tpu_custom_call" | custom-call | flops 8699904 | bytes 4349952 | tf_op jit(solution)/shard_map/pallas_call | solution.py:532
  36.2 0.0 all-to-all-done.copies
  36.2 0.5 %shard_map.66 = f32[1,128]{1,0:T(1,128)} custom-call(f32[32,1,128]{2,1,0:T(1,128)S(1)} %all-to-all-done.copies), custom_call_target="tpu_custom_call" | custom-call | flops 33792 | bytes 16896 | tf_op jit(solution)/shard_map/pallas_call | solution.py:532
Async XLA Ops:
  0.6 1.5 %copy-start = (f32[26,8,16,128]{3,2,1,0:T(8,128)S(1)}, f32[26,8,16,128]{3,2,1,0:T(8,128)}, u32[]{:S(2)}) copy-start(f32[26,8,16,128]{3,2,1,0:T(8,128)} %adjoint.5) | copy-start | bytes 5111812
  2.1 9.7 %copy-start.1 = (f32[26,8,16,128]{3,2,1,0:T(8,128)S(1)}, f32[26,8,16,128]{3,2,1,0:T(8,128)}, u32[]{:S(2)}) copy-start(f32[26,8,16,128]{3,2,1,0:T(8,128)} %adjoint.5) | copy-start | bytes 5111812
  2.3 9.5 %collective-permute-start = (f32[7,8,128]{2,1,0:T(8,128)S(1)}, f32[7,8,128]{2,1,0:T(8,128)S(1)}, u32[]{:S(2)}, u32[]{:S(2)}) collective-permute-start(f32[7,8,128]{2,1,0:T(8,128)S(1)} %get-tuple-element.14), channel_id=1, source_target_pairs={{0,1},{1,0},{2,3},{3,2},{4,5},{5,4},{6,7},{7,6},{8,9},{9,8},{10,11... | collective-permute-start | bytes 86024 | tf_op jit(solution)/shard_map/ppermute | solution.py:557
  2.3 9.4 %collective-permute-start.1 = (f32[7,8,128]{2,1,0:T(8,128)S(1)}, f32[7,8,128]{2,1,0:T(8,128)S(1)}, u32[]{:S(2)}, u32[]{:S(2)}) collective-permute-start(f32[7,8,128]{2,1,0:T(8,128)S(1)} %get-tuple-element.15), channel_id=1, source_target_pairs={{1,2},{2,1},{5,6},{6,5},{9,10},{10,9},{13,14},{14,13},{17,18},{18,... | collective-permute-start | bytes 86024 | tf_op jit(solution)/shard_map/ppermute | solution.py:557
  7.0 1.5 %copy-start.2 = (f32[26,8,16,128]{3,2,1,0:T(8,128)S(1)}, f32[26,8,16,128]{3,2,1,0:T(8,128)}, u32[]{:S(2)}) copy-start(f32[26,8,16,128]{3,2,1,0:T(8,128)} %primal.3) | copy-start | bytes 5111812
  8.4 0.8 %copy-start.3 = (s32[8,16,128]{2,1,0:T(8,128)S(1)}, s32[8,16,128]{2,1,0:T(8,128)}, u32[]{:S(2)}) copy-start(s32[8,16,128]{2,1,0:T(8,128)} %solid.1) | copy-start | bytes 196612
  9.3 0.8 %copy-start.4 = (s32[3,1,2464]{2,1,0:T(1,128)S(1)}, s32[3,1,2464]{2,1,0:T(1,128)}, u32[]{:S(2)}) copy-start(s32[3,1,2464]{2,1,0:T(1,128)} %links.1) | copy-start | bytes 88708
  12.1 6.1 %collective-permute-start.2 = (f32[280,128]{1,0:T(8,128)S(1)}, f32[280,128]{1,0:T(8,128)S(1)}, u32[]{:S(2)}, u32[]{:S(2)}) collective-permute-start(f32[280,128]{1,0:T(8,128)S(1)} %get-tuple-element.18), channel_id=1, source_target_pairs={{0,4},{4,0},{8,12},{12,8},{16,20},{20,16},{24,28},{28,24},{1,5},{5... | collective-permute-start | bytes 430088 | tf_op jit(solution)/shard_map/ppermute | solution.py:557
  13.4 6.6 %collective-permute-start.3 = (f32[280,128]{1,0:T(8,128)S(1)}, f32[280,128]{1,0:T(8,128)S(1)}, u32[]{:S(2)}, u32[]{:S(2)}) collective-permute-start(f32[280,128]{1,0:T(8,128)S(1)} %get-tuple-element.19), channel_id=1, source_target_pairs={{4,8},{8,4},{12,16},{16,12},{20,24},{24,20},{28,0},{0,28},{5,9},{9... | collective-permute-start | bytes 430088 | tf_op jit(solution)/shard_map/ppermute | solution.py:557
  22.8 13.4 %all-to-all-start = ((f32[32,1,128]{2,1,0:T(1,128)}), f32[32,1,128]{2,1,0:T(1,128)S(1)}, u32[]{:S(2)}, u32[]{:S(2)}) async-start(f32[32,1,128]{2,1,0:T(1,128)} %shard_map.65), calls=%async_computation | async-start | bytes 32768 | tf_op jit(solution)/shard_map/all_to_all | solution.py:636
  28.2 3.7 %collective-permute-start.4 = (f32[7,8,128]{2,1,0:T(8,128)S(1)}, f32[7,8,128]{2,1,0:T(8,128)S(1)}, u32[]{:S(2)}, u32[]{:S(2)}) collective-permute-start(f32[7,8,128]{2,1,0:T(8,128)S(1)} %get-tuple-element.23), channel_id=1, source_target_pairs={{0,1},{1,0},{2,3},{3,2},{4,5},{5,4},{6,7},{7,6},{8,9},{9,8},{10,11... | collective-permute-start | bytes 86024 | tf_op jit(solution)/shard_map/ppermute | solution.py:557
  28.5 5.5 %collective-permute-start.5 = (f32[7,8,128]{2,1,0:T(8,128)S(1)}, f32[7,8,128]{2,1,0:T(8,128)S(1)}, u32[]{:S(2)}, u32[]{:S(2)}) collective-permute-start(f32[7,8,128]{2,1,0:T(8,128)S(1)} %get-tuple-element.24), channel_id=1, source_target_pairs={{1,2},{2,1},{5,6},{6,5},{9,10},{10,9},{13,14},{14,13},{17,18},{18,... | collective-permute-start | bytes 86024 | tf_op jit(solution)/shard_map/ppermute | solution.py:557
